TPU v7x, 512 devices: a whole 4x4x16 slice. The times are simulated.
512 devices in a mesh: front: 128 (over x, z, core), chain: 4 (over y).
Axes of the slice: x: 4, y: 4, z: 16, core: 2. Of those that a mesh axis runs over, the one named last changes fastest.
Arguments:
- rhs: float32 [131072, 128], P(('front', 'chain')), may hold values from -6 to 6
- child_blocks: bfloat16 [45056, 128, 128], P(('front', 'chain')), may hold values from -4 to 4
- dest_front: int32 [45056, 1], P(('front', 'chain')), may hold values from 0 to 127; in each aligned block of 88 rows (0 to 87, 88 to 175, ...) at most 2 rows name the same one
- dest_place: int32 [45056], P(('front', 'chain')), may hold values from -4 to 23
- front_pivots: int32 [128], P('front'), may hold values from 512 to 1024, as said below
- diag_inv: float32 [131072, 256], P(('front', 'chain')), as said below
- lower_factor: bfloat16 [131072, 768], P(('front', 'chain')), may hold values from -0.1875 to 0.1875
- update_factor: bfloat16 [262144, 1024], P(('front', 'chain')), may hold values from -0.1875 to 0.1875
Outputs:
- solution: float32 [131072, 128], P(('front', 'chain'))
- update_out: float32 [262144, 128], P(('front', 'chain'))
Inputs may be any that keep to these rules, and one draw needn't show every extreme that they name: `dest_front`: at most 2 of the 88 blocks of one device go to one front, and that many do in every draw. `front_pivots`: pivot rows at or beyond this count are padding and solve to zero; some front has all 1024. `diag_inv`: each 256 by 256 block is lower triangular with its diagonal between 0.4 and 1.6.
All inputs are finite; a program needn't handle non-finite values.
Results may differ from a plain program's by a relative error of at most 0.0027.
Values may be sent and summed in bfloat16 or wider, within the bound.
No kernel may reach another device: no remote copies, remote signals or barrier semaphores. Data moves between devices by JAX's collectives and lax.ppermute only.
A program may use at most 64 MiB of HBM per device.

v0:
```python
import jax
import jax.numpy as jnp
from jax import lax
from jax.sharding import PartitionSpec as P

BR = 128


def broadcast(value, axis, source):
    kept = jnp.where(lax.axis_index(axis) == source, value, 0).astype(value.dtype)
    return lax.psum(kept, axis)


def slot_table(blocks, fronts, places, dest_count, slot_width):
    block_count = fronts.shape[0]
    sequence = jnp.arange(block_count, dtype=jnp.int32)
    earlier = (fronts[None, :] == fronts[:, None]) & (sequence[None, :] < sequence[:, None])
    rank_of = jnp.sum(earlier.astype(jnp.int32), axis=1)
    target = fronts * slot_width + rank_of
    source = jnp.full((dest_count * slot_width,), block_count, jnp.int32).at[target].set(sequence)
    slot_data = jnp.take(blocks, source, axis=0, mode="fill", fill_value=0)
    labels = jnp.take(places, source, axis=0, mode="fill", fill_value=-1)
    return (
        slot_data.reshape((dest_count, slot_width) + blocks.shape[1:]),
        labels.reshape(dest_count, slot_width),
    )


def assemble(slot_data, labels, piv_blocks, upd_blocks, owners):
    flattened = slot_data.reshape((-1,) + slot_data.shape[2:])
    tag_list = labels.reshape(-1)
    per_owner = piv_blocks + upd_blocks
    first_update = piv_blocks * owners
    update_index = tag_list - first_update
    placed = jnp.where(
        tag_list < first_update,
        tag_list // piv_blocks * per_owner + tag_list % piv_blocks,
        update_index // upd_blocks * per_owner + piv_blocks + update_index % upd_blocks,
    )
    placed = jnp.where(tag_list < 0, -1, placed)
    row_ids = jnp.arange(owners * per_owner, dtype=jnp.int32)
    onehot = (placed[None, :] == row_ids[:, None]).astype(jnp.bfloat16)
    return jnp.einsum("km,mrs->krs", onehot, flattened, preferred_element_type=jnp.float32)


def body(
    rhs, child_blocks, dest_front, dest_place, front_pivots, diag_inv, lower_factor, update_factor
):
    owners = lax.axis_size("chain")
    front_count = lax.axis_size("front")
    chain_at = lax.axis_index("chain")
    piv_rows = rhs.shape[0]
    upd_rows = update_factor.shape[0]
    source_width = rhs.shape[1]
    piv_blocks = piv_rows // BR
    upd_blocks = upd_rows // BR
    per_device = child_blocks.shape[0]
    capacity = max(2, (per_device + front_count - 1) // front_count * 2)
    slot_data, labels = slot_table(
        child_blocks, dest_front[:, 0], dest_place, front_count, capacity
    )
    received, received_labels = (
        lax.all_to_all(slot_data, "front", split_axis=0, concat_axis=0, tiled=True),
        lax.all_to_all(labels, "front", split_axis=0, concat_axis=0, tiled=True),
    )
    merged = assemble(received, received_labels, piv_blocks, upd_blocks, owners)
    owned = lax.psum_scatter(merged, "chain", scatter_dimension=0, tiled=True)
    pivot_rhs = rhs + owned[:piv_blocks].reshape(piv_rows, source_width)
    update_start = owned[piv_blocks:].reshape(upd_rows, source_width)
    positions = chain_at * piv_rows + jnp.arange(piv_rows, dtype=jnp.int32)
    live_rows = (positions < front_pivots[0]).astype(jnp.float32)[:, None]
    running = pivot_rhs
    updates = update_start
    solved = jnp.zeros_like(pivot_rhs)
    for section in range(owners):
        candidate = live_rows * jnp.dot(diag_inv, running, precision=lax.Precision.HIGHEST)
        solved = jnp.where(chain_at == section, candidate, solved)
        solved_bf = broadcast(candidate.astype(jnp.bfloat16), "chain", section)
        advance_running = running
        advance_updates = updates
        if section < owners - 1:
            factor_block = lower_factor[:, section * piv_rows : (section + 1) * piv_rows]
            product = jnp.dot(factor_block, solved_bf, preferred_element_type=jnp.float32)
            advance_running = advance_running - jnp.where(chain_at > section, product, 0.0)
        update_block = update_factor[:, section * piv_rows : (section + 1) * piv_rows]
        advance_updates = advance_updates - jnp.dot(
            update_block, solved_bf, preferred_element_type=jnp.float32
        )
        running = advance_running
        updates = advance_updates
    return (solved, updates)


def solution(mesh):
    return jax.shard_map(
        body,
        mesh=mesh,
        in_specs=(
            P(("front", "chain"), None),
            P(("front", "chain"), None, None),
            P(("front", "chain"), None),
            P(("front", "chain")),
            P("front"),
            P(("front", "chain"), None),
            P(("front", "chain"), None),
            P(("front", "chain"), None),
        ),
        out_specs=(P(("front", "chain"), None), P(("front", "chain"), None)),
        check_vma=False,
    )
```

profile of v0, /device:TPU:6, one launch (start us, length us, event | category | flops | bytes accessed | tf_op | source)
XLA Modules:
  0.0 734.4 jit_solution(3407166581159611724)
XLA Ops:
  7.2 1.0 convert_reduce_fusion
  8.9 0.8 scatter_custom_fusion
  9.7 1.9 gather_fusion
  11.6 0.8 select_n.170
  12.4 19.9 %all-to-all-start = ((s32[128,1,2]{2,1,0:T(1,128)}), s32[128,1,2]{2,1,0:T(1,128)S(1)}, u32[]{:S(2)}, u32[]{:S(2)}) async-start(s32[128,1,2]{2,1,0:T(1,128)} %bitcast.4), calls=%async_computation | async-start | bytes 131072 | tf_op jit(solution)/shard_map/all_to_all | solution.py:64
  32.5 8.4 %gather_fusion.1 = bf16[256,128,128]{2,1,0:T(8,128)(2,1)} fusion(bf16[88,128,128]{2,1,0:T(8,128)(2,1)S(1)} %copy-done, s32[1024]{0:T(1024)S(1)} %pad_clamp_fusion), kind=kCustom, calls=%fused_computation.1 | custom fusion | bytes 16778240 | tf_op jit(solution)/shard_map/jit(_take)/gather | solution.py:21
  40.9 7.3 broadcast_select_fusion
  48.2 16.3 %copy.40 = bf16[128,2,128,128]{3,1,2,0:T(2,128)(2,1)} copy(bf16[128,2,128,128]{3,2,1,0:T(8,128)(2,1)} %broadcast_select_fusion) | data formatting | bytes 16777216 | tf_op jit(solution)/shard_map/jit(_take)/select_n | solution.py:21
  64.5 16.7 %all-to-all-start.1 = ((bf16[128,2,128,128]{3,1,2,0:T(2,128)(2,1)}), bf16[128,2,128,128]{3,1,2,0:T(2,128)(2,1)}, u32[]{:S(2)}, u32[]{:S(2)}) async-start(bf16[128,2,128,128]{3,1,2,0:T(2,128)(2,1)} %copy.40), calls=%async_computation.1 | async-start | bytes 16777216 | tf_op jit(solution)/shard_map/all_to_all | solution.py:63
  81.7 0.8 reduce.3
  82.7 363.2 %all-to-all-done.1 = bf16[128,2,128,128]{3,1,2,0:T(2,128)(2,1)} async-done(((bf16[128,2,128,128]{3,1,2,0:T(2,128)(2,1)}), bf16[128,2,128,128]{3,1,2,0:T(2,128)(2,1)}, u32[]{:S(2)}, u32[]{:S(2)}) %all-to-all-start.1) | async-done | bytes 8388640 | tf_op jit(solution)/shard_map/all_to_all | solution.py:63
  445.9 7.3 copy.41
  453.3 1.2 fusion.19
  454.4 1.5 copy.42
  456.9 29.3 %reduce-scatter.2.cloned.1.call-done = f32[6,128,128]{2,1,0:T(8,128)} async-done(((f32[24,128,128]{2,1,0:T(8,128)}), f32[6,128,128]{2,1,0:T(8,128)}) %reduce-scatter.2.cloned.1.call-update) | async-done | bytes 393232 | tf_op jit(solution)/shard_map/reduce_scatter | solution.py:67
  486.3 0.9 slice.40
  488.5 1.7 slice.41
  490.2 1.8 copy.45
  491.9 53.7 %all-reduce.5.cloned.1.call-done = bf16[256,128]{0,1:T(8,128)(2,1)} async-done(((bf16[256,128]{0,1:T(8,128)(2,1)}), bf16[256,128]{0,1:T(8,128)(2,1)}) %all-reduce.5.cloned.1.call-update) | async-done | bytes 65552 | tf_op jit(solution)/shard_map/psum | solution.py:11
  545.6 1.1 fusion.9
  547.9 2.0 fusion.3
  549.9 55.7 %all-reduce.7.cloned.1.call-done = bf16[256,128]{0,1:T(8,128)(2,1)} async-done(((bf16[256,128]{0,1:T(8,128)(2,1)}), bf16[256,128]{0,1:T(8,128)(2,1)}) %all-reduce.7.cloned.1.call-update) | async-done | bytes 65552 | tf_op jit(solution)/shard_map/psum | solution.py:11
  605.6 1.1 fusion.7
  608.5 2.0 fusion.2
  610.5 55.2 %all-reduce.9.cloned.1.call-done = bf16[256,128]{0,1:T(8,128)(2,1)} async-done(((bf16[256,128]{0,1:T(8,128)(2,1)}), bf16[256,128]{0,1:T(8,128)(2,1)}) %all-reduce.9.cloned.1.call-update) | async-done | bytes 65552 | tf_op jit(solution)/shard_map/psum | solution.py:11
  665.7 1.2 fusion.5
  668.6 1.3 fusion.1
  669.9 0.7 select_bitcast_fusion
  670.6 1.7 copy.46
  672.3 53.6 %all-reduce.11.cloned.1.call-done = bf16[256,128]{0,1:T(8,128)(2,1)} async-done(((bf16[256,128]{0,1:T(8,128)(2,1)}), bf16[256,128]{0,1:T(8,128)(2,1)}) %all-reduce.11.cloned.1.call-update) | async-done | bytes 65552 | tf_op jit(solution)/shard_map/psum | solution.py:11
  725.8 1.2 fusion
  727.0 0.8 copy.47
  (42 shorter events, 7.7 us)
Async XLA Ops:
  7.2 25.3 %copy-start = (bf16[88,128,128]{2,1,0:T(8,128)(2,1)S(1)}, bf16[88,128,128]{2,1,0:T(8,128)(2,1)}, u32[]{:S(2)}) copy-start(bf16[88,128,128]{2,1,0:T(8,128)(2,1)} %param.9) | copy-start | bytes 8650756
  12.4 52.0 %all-to-all-start = ((s32[128,1,2]{2,1,0:T(1,128)}), s32[128,1,2]{2,1,0:T(1,128)S(1)}, u32[]{:S(2)}, u32[]{:S(2)}) async-start(s32[128,1,2]{2,1,0:T(1,128)} %bitcast.4), calls=%async_computation | async-start | bytes 131072 | tf_op jit(solution)/shard_map/all_to_all | solution.py:64
  64.5 381.5 %all-to-all-start.1 = ((bf16[128,2,128,128]{3,1,2,0:T(2,128)(2,1)}), bf16[128,2,128,128]{3,1,2,0:T(2,128)(2,1)}, u32[]{:S(2)}, u32[]{:S(2)}) async-start(bf16[128,2,128,128]{3,1,2,0:T(2,128)(2,1)} %copy.40), calls=%async_computation.1 | async-start | bytes 16777216 | tf_op jit(solution)/shard_map/all_to_all | solution.py:63
  81.1 405.2 %reduce-scatter.2.cloned.1.call-start = ((), (), s32[]{:S(2)}) async-start(), calls=%async_computation.3 | async-start | bytes 1966080 | tf_op jit(solution)/shard_map/reduce_scatter | solution.py:67
  453.2 2.9 copy-start.4
  453.2 34.1 %copy-start.1 = (f32[256,256]{1,0:T(8,128)S(1)}, f32[256,256]{1,0:T(8,128)}, u32[]{:S(2)}) copy-start(f32[256,256]{1,0:T(8,128)} %param.13) | copy-start | bytes 786436
  455.9 89.7 %all-reduce.5.cloned.1.call-start = ((), (), s32[]{:S(2)}) async-start(), calls=%async_computation.4 | async-start | bytes 131072 | tf_op jit(solution)/shard_map/psum | solution.py:11
  488.4 117.2 %all-reduce.7.cloned.1.call-start = ((), (), s32[]{:S(2)}) async-start(), calls=%async_computation.5 | async-start | bytes 131072 | tf_op jit(solution)/shard_map/psum | solution.py:11
  547.8 117.8 %all-reduce.9.cloned.1.call-start = ((), (), s32[]{:S(2)}) async-start(), calls=%async_computation.6 | async-start | bytes 131072 | tf_op jit(solution)/shard_map/psum | solution.py:11
  606.7 0.7 copy-start.3
  608.5 117.4 %all-reduce.11.cloned.1.call-start = ((), (), s32[]{:S(2)}) async-start(), calls=%async_computation.7 | async-start | bytes 131072 | tf_op jit(solution)/shard_map/psum | solution.py:11
  667.3 0.7 copy-start.2
Sparse Core Ops, SparseCore 0:
  456.1 30.1 reduce-scatter.1
  489.2 56.4 all-reduce.4
  548.5 57.0 all-reduce.6
  608.6 57.0 all-reduce.8
  668.7 57.0 all-reduce.10
where the time goes:
time: 735 us; the launch traced here: 734 us
  waiting for transfers between devices  611 us (83%)
  local copies, waits for them, and re-layouts  46.1 us (6%)
  starting transfers between devices  37 us (5%)
  between operations  14.7 us (2%)
  other arithmetic  13.1 us (2%)
  matrix products  12.8 us (2%)
    all_to_all x1, waiting for transfers between devices, body(): lax.all_to_all(slot_data, 'front', split_axis=0, concat_axis=0, tiled=True)  363 us
    psum x4, waiting for transfers between devices, broadcast(): return lax.psum(kept, axis)  218 us
    reduce_scatter x1, waiting for transfers between devices, body(): owned = lax.psum_scatter(merged, 'chain', scatter_dimension=0, tiled=True)  29.3 us
    all_to_all x1, starting transfers between devices, body(): lax.all_to_all(labels, 'front', split_axis=0, concat_axis=0, tiled=True)  19.9 us
    all_to_all x1, starting transfers between devices, body(): lax.all_to_all(slot_data, 'front', split_axis=0, concat_axis=0, tiled=True)  16.7 us
    select_n x1, local copies, waits for them, and re-layouts, slot_table(): slot_data = jnp.take(blocks, source, axis=0, mode='fill', fill_value=0)  16.3 us
  transfers between devices with their start and end apart: 7, of which 6 were waited for; matrix products, arithmetic and copies ran while one was open for 6% of the time, Pallas kernels for 0%

commit v1 on v0

v1 whole, which is shorter than its diff:
```python
import jax
import jax.numpy as jnp
from jax import lax
from jax.experimental import pallas as pl
from jax.experimental.pallas import tpu as pltpu
from jax.sharding import Mesh, PartitionSpec as P

BR = 128
FRONT = ("x", "z", "core")
ALL = ("x", "z", "core", "chain")
SLAB = ("x", "core", "chain")
SLOTS = 11
PEERS = 32
LABEL_ROWS = 16
OWNED = 6


def slot_table(blocks, fronts, places, dest_count, slot_width):
    block_count = fronts.shape[0]
    sequence = jnp.arange(block_count, dtype=jnp.int32)
    earlier = (fronts[None, :] == fronts[:, None]) & (sequence[None, :] < sequence[:, None])
    rank_of = jnp.sum(earlier.astype(jnp.int32), axis=1)
    target = fronts * slot_width + rank_of
    source = jnp.full((dest_count * slot_width,), block_count, jnp.int32).at[target].set(sequence)
    slot_data = jnp.take(blocks, source, axis=0, mode="fill", fill_value=0)
    labels = jnp.take(places, source, axis=0, mode="fill", fill_value=-1)
    return (
        slot_data.reshape((dest_count, slot_width) + blocks.shape[1:]),
        labels.reshape(dest_count, slot_width),
    )


def full_exchange(child_blocks, fronts, places):
    slot_data, labels = slot_table(child_blocks, fronts, places, 128, 2)
    received = lax.all_to_all(slot_data, FRONT, split_axis=0, concat_axis=0, tiled=True)
    tags = lax.all_to_all(labels, FRONT, split_axis=0, concat_axis=0, tiled=True).reshape(-1)
    placed = jnp.where(
        tags < 8, tags // 2 * OWNED + tags % 2, (tags - 8) // 4 * OWNED + 2 + (tags - 8) % 4
    )
    placed = jnp.where(tags < 0, -1, placed)
    row_ids = jnp.arange(4 * OWNED, dtype=jnp.int32)
    onehot = (placed[None, :] == row_ids[:, None]).astype(jnp.bfloat16)
    flattened = received.reshape((-1,) + received.shape[2:])
    merged = jnp.einsum("km,mrs->krs", onehot, flattened, preferred_element_type=jnp.float32)
    return lax.psum_scatter(merged, "chain", scatter_dimension=0, tiled=True)


def send_kernel(front, place, blocks, out, over, marks, tags, counts, sem, tag_sem):
    for peer in range(PEERS):
        counts[peer] = 0
    marks[...] = jnp.full(marks.shape, -1.0, jnp.float32)
    lane = lax.broadcasted_iota(jnp.int32, (8, 128), 1)

    def step(i, carry):
        missed, sent = carry
        where_front = front[i]
        spot = place[i]
        live = spot >= 0
        pivot = spot < 8
        owner = jnp.where(pivot, spot >> 1, (spot - 8) >> 2)
        peer = ((where_front >> 5) * 2 + (where_front & 1)) * 4 + owner
        peer = jnp.where(live, peer, 0)
        index = ((where_front >> 1) & 15) * OWNED + jnp.where(pivot, spot & 1, 2 + ((spot - 8) & 3))
        used = counts[peer]
        fits = live & (used < SLOTS)

        @pl.when(fits)
        def _():
            counts[peer] = used + 1
            pltpu.make_async_copy(
                blocks.at[i], out.at[peer, pl.ds(pl.multiple_of(used * BR, BR), BR)], sem
            ).start()
            marks[peer] = jnp.where(lane == used, index.astype(jnp.float32), marks[peer])

        return (
            missed + jnp.where(live & (used >= SLOTS), 1, 0),
            sent + jnp.where(fits, 1, 0),
        )

    missed, sent = lax.fori_loop(0, front.shape[0], step, (jnp.int32(0), jnp.int32(0)))
    over[0] = missed
    half = marks[...].astype(jnp.bfloat16)
    tags[:, 0:8, :] = half
    tags[:, 8:16, :] = half
    tag_copy = pltpu.make_async_copy(tags, out.at[:, pl.ds(SLOTS * BR, LABEL_ROWS)], tag_sem)
    tag_copy.start()

    def drain(i, carry):
        pltpu.make_async_copy(blocks.at[0], out.at[0, pl.ds(0, BR)], sem).wait()
        return carry

    lax.fori_loop(0, sent, drain, 0)
    tag_copy.wait()


def pack(fronts, places, blocks):
    return pl.pallas_call(
        send_kernel,
        out_shape=(
            jax.ShapeDtypeStruct((PEERS, SLOTS * BR + LABEL_ROWS, 128), jnp.bfloat16),
            jax.ShapeDtypeStruct((1,), jnp.int32),
        ),
        in_specs=[
            pl.BlockSpec(memory_space=pltpu.SMEM),
            pl.BlockSpec(memory_space=pltpu.SMEM),
            pl.BlockSpec(memory_space=pl.ANY),
        ],
        out_specs=(pl.BlockSpec(memory_space=pl.ANY), pl.BlockSpec(memory_space=pltpu.SMEM)),
        scratch_shapes=[
            pltpu.VMEM((PEERS, 8, 128), jnp.float32),
            pltpu.VMEM((PEERS, LABEL_ROWS, 128), jnp.bfloat16),
            pltpu.SMEM((PEERS,), jnp.int32),
            pltpu.SemaphoreType.DMA,
            pltpu.SemaphoreType.DMA,
        ],
        name="pack",
    )(fronts, places, blocks)


def gather_kernel(index, block, out):
    source = pl.program_id(0)

    @pl.when(source == 0)
    def _():
        out[...] = jnp.zeros(out.shape, jnp.float32)

    for slot in range(SLOTS):
        target = index[source * SLOTS + slot]

        @pl.when(target >= 0)
        def _():
            out[target] += block[0, slot * BR : (slot + 1) * BR, :].astype(jnp.float32)


def add_up(index, received):
    rows = received.shape[1]
    return pl.pallas_call(
        gather_kernel,
        out_shape=jax.ShapeDtypeStruct((16 * OWNED, BR, 128), jnp.float32),
        grid_spec=pltpu.PrefetchScalarGridSpec(
            num_scalar_prefetch=1,
            grid=(PEERS,),
            in_specs=[pl.BlockSpec((1, rows, 128), lambda i, ids: (i, 0, 0))],
            out_specs=pl.BlockSpec((16 * OWNED, BR, 128), lambda i, ids: (0, 0, 0)),
        ),
        name="add_up",
    )(index, received)


def solve_kernel(spot, pivots, rhs, lower, inverse, owned, update, solved_out, update_out, kept):
    chain_at = spot[0]
    live_count = pivots[0]
    for block in range(4):
        rows = slice(block * 256, (block + 1) * 256)
        partial = rhs[rows, :]
        if block > 0:
            partial = partial - jnp.dot(
                lower[rows, 0 : block * 256],
                kept[0 : block * 256, :],
                preferred_element_type=jnp.float32,
            )
        row = block * 256 + lax.broadcasted_iota(jnp.int32, (256, 128), 0)
        product = jnp.dot(
            inverse[rows, :],
            partial,
            precision=lax.Precision.HIGHEST,
            preferred_element_type=jnp.float32,
        )
        here = jnp.where(row < live_count, product, 0.0)
        kept[rows, :] = here.astype(jnp.bfloat16)

        @pl.when(chain_at == block)
        def _():
            solved_out[...] = here

    update_out[...] = owned[256:768, :] - jnp.dot(
        update[...], kept[...], preferred_element_type=jnp.float32
    )


def solve(spot, pivots, rhs, lower, inverse, owned, update):
    smem = pl.BlockSpec(memory_space=pltpu.SMEM)
    vmem = pl.BlockSpec(memory_space=pltpu.VMEM)
    return pl.pallas_call(
        solve_kernel,
        out_shape=(
            jax.ShapeDtypeStruct((256, 128), jnp.float32),
            jax.ShapeDtypeStruct((512, 128), jnp.float32),
        ),
        in_specs=[smem, smem, vmem, vmem, vmem, vmem, vmem],
        out_specs=(vmem, vmem),
        scratch_shapes=[pltpu.VMEM((1024, 128), jnp.bfloat16)],
        name="solve",
    )(spot, pivots, rhs, lower, inverse, owned, update)


def body(
    rhs, child_blocks, dest_front, dest_place, front_pivots, diag_inv, lower_factor, update_factor
):
    fronts = dest_front.reshape(-1)
    packed, over = pack(fronts, dest_place, child_blocks)
    overflow = lax.pmax(over, ALL)
    received = lax.all_to_all(packed, SLAB, split_axis=0, concat_axis=0, tiled=True)
    index = received[:, SLOTS * BR, :SLOTS].astype(jnp.int32).reshape(-1)
    dense = add_up(index, received)
    owned = lax.psum_scatter(dense, "z", scatter_dimension=0, tiled=True)
    owned = lax.cond(
        overflow[0] > 0,
        lambda fast: full_exchange(child_blocks, fronts, dest_place),
        lambda fast: fast,
        owned,
    )
    owned = owned.reshape(OWNED * BR, 128)
    all_lower = lax.all_gather(lower_factor, "chain", axis=0, tiled=True)
    all_inverse = lax.all_gather(diag_inv, "chain", axis=0, tiled=True)
    all_rhs = lax.all_gather(rhs + owned[:256], "chain", axis=0, tiled=True)
    spot = lax.axis_index("chain").astype(jnp.int32).reshape(1)
    return solve(spot, front_pivots, all_rhs, all_lower, all_inverse, owned, update_factor)


def solution(mesh):
    grid = Mesh(mesh.devices.reshape(4, 16, 2, 4), ALL)
    rows = P(ALL, None)
    return jax.shard_map(
        body,
        mesh=grid,
        in_specs=(rows, P(ALL, None, None), rows, P(ALL), P(FRONT), rows, rows, rows),
        out_specs=(rows, rows),
        check_vma=False,
    )
```

time: 735 us -> 450 us (0.61)
  waiting for transfers between devices: 611 us -> 49.7 us
  blocking collectives: 0 us -> 269 us
  Pallas kernels: 0 us -> 105 us
  local copies, waits for them, and re-layouts: 46.1 us -> 7.57 us
  starting transfers between devices: 37 us -> 0.08 us
  other arithmetic: 13.1 us -> 0.07 us
  matrix products: 12.8 us -> 0 us
    all_to_all x2 -> x0, waiting for transfers between devices: 363 us -> none  [the longest x1 363 us: body(): lax.all_to_all(slot_data, 'front', split_axis=0, concat_axis=0, tiled=True)]
    psum x4 -> x0, waiting for transfers between devices: 218 us -> none  [broadcast(): return lax.psum(kept, axis)]
    all_to_all x0 -> x1, blocking collectives: none -> 141 us  [body(): lax.all_to_all(packed, SLAB, split_axis=0, concat_axis=0, tiled=True)]
    pmax x0 -> x1, blocking collectives: none -> 114 us  [body(): overflow = lax.pmax(over, ALL)]
    pallas_call x0 -> x3, Pallas kernels: none -> 105 us  [the longest x1 76.8 us: pack(): pl.pallas_call(send_kernel, out_shape=(jax.ShapeDtypeStruct((PEERS, SLOTS...]
    all_gather x0 -> x2, waiting for transfers between devices: none -> 48.6 us  [the longest x1 36.5 us: body(): all_lower = lax.all_gather(lower_factor, 'chain', axis=0, tiled=True)]
    all_to_all x2 -> x0, starting transfers between devices: 36.6 us -> none  [the longest x1 19.9 us: body(): lax.all_to_all(labels, 'front', split_axis=0, concat_axis=0, tiled=True)]
    reduce_scatter x1, waiting for transfers between devices: 29.3 us -> 0.02 us  [body(): owned = lax.psum_scatter(dense, 'z', scatter_dimension=0, tiled=True)]
  transfers between devices with their start and end apart: 7 -> 3, of which waited for: 6 -> 2; matrix products, arithmetic and copies ran while one was open for 6% -> 0% of each run, Pallas kernels for 0% -> 0%
where the time goes in v1:
time: 450 us; the launch traced here: 448 us
  blocking collectives  269 us (60%)
  Pallas kernels  105 us (23%)
  waiting for transfers between devices  49.7 us (11%)
  between operations  16.8 us (4%)
  local copies, waits for them, and re-layouts  7.57 us (2%)
    all_to_all x1, blocking collectives, body(): lax.all_to_all(packed, SLAB, split_axis=0, concat_axis=0, tiled=True)  141 us
    pmax x1, blocking collectives, body(): overflow = lax.pmax(over, ALL)  114 us
    pallas_call x1, Pallas kernels, pack(): pl.pallas_call(send_kernel, out_shape=(jax.ShapeDtypeStruct((PEERS, SLOTS...  76.8 us
    all_gather x1, waiting for transfers between devices, body(): all_lower = lax.all_gather(lower_factor, 'chain', axis=0, tiled=True)  36.5 us
    pallas_call x1, Pallas kernels, add_up(): pl.pallas_call(gather_kernel, out_shape=jax.ShapeDtypeStruct((16 * OWNED,...  21.6 us
    all_gather x1, blocking collectives, body(): all_rhs = lax.all_gather(rhs + owned[:256], 'chain', axis=0, tiled=True)  14.2 us
    all_gather x1, waiting for transfers between devices, body(): all_inverse = lax.all_gather(diag_inv, 'chain', axis=0, tiled=True)  12.1 us
  transfers between devices with their start and end apart: 3, of which 2 were waited for; matrix products, arithmetic and copies ran while one was open for 0% of the time, Pallas kernels for 0%

profile of v1, /device:TPU:6, one launch (start us, length us, event | category | flops | bytes accessed | tf_op | source)
XLA Modules:
  0.0 448.0 jit_solution(13233779907937508794)
XLA Ops:
  8.0 0.0 reduce-scatter.5.cloned.1.call-start
  8.0 76.8 %pack.1 = (bf16[32,1424,128]{2,1,0:T(8,128)(2,1)}, s32[1]{0:T(128)}) custom-call(s32[88]{0:T(128)} %bitcast.17, s32[88]{0:T(128)} %place.1, bf16[88,128,128]{2,1,0:T(8,128)(2,1)} %blocks.1), custom_call_target="tpu_custom_call" | custom-call | tf_op jit(solution)/shard_map/pack/pallas_call | solution.py:97
  84.8 141.2 %all_to_all.14.block = bf16[32,1424,128]{2,1,0:T(8,128)(2,1)S(1)} all-to-all(bf16[32,1424,128]{2,1,0:T(8,128)(2,1)} %get-tuple-element.32), channel_id=1, replica_groups=mesh['x'=4,'z'=16,'core'=2,'chain'=4] {'x','core','chain'}, dimensions={0} | all-to-all | bytes 23330816 | tf_op jit(solution)/shard_map/all_to_all | solution.py:203
  226.1 0.0 copy-start.1
  226.1 4.4 copy-done.1
  230.4 0.1 fusion.10
  230.5 0.7 reshape.163.index
  231.2 0.0 copy-start
  231.2 0.0 copy-start.2
  231.2 0.0 copy-start.4
  231.2 21.6 %add_up.1 = f32[96,128,128]{2,1,0:T(8,128)} custom-call(s32[352]{0:T(512)} %reshape.163.index, bf16[32,1424,128]{2,1,0:T(8,128)(2,1)} %copy-done.1), custom_call_target="tpu_custom_call" | custom-call | tf_op jit(solution)/shard_map/add_up/pallas_call | solution.py:137
  252.8 0.0 reduce-scatter.5.cloned.1.call-update
  252.8 113.5 %pmax.7 = s32[1]{0:T(128)} all-reduce(s32[1]{0:T(128)} %get-tuple-element.31), channel_id=1, replica_groups=mesh['x'=4,'z'=16,'core'=2,'chain'=4] {'x','z','core','chain'}, use_global_device_ids=true, to_apply=%region_0.0 | all-reduce | flops 1 | bytes 8 | tf_op jit(solution)/shard_map/pmax | solution.py:202
  367.0 0.0 reduce-scatter.5.cloned.1.call-done
  367.1 0.0 copy-done
  367.1 0.0 copy-done.2
  367.1 0.0 copy-done.4
  367.1 0.0 copy-start.3
  367.1 2.5 conditional.1
  367.1 1.6 slice.12
  368.7 0.9 copy.39
  369.6 0.0 all-gather.5.cloned.1.call-start
  369.6 0.6 all-gather.5.cloned.1.call-update
  370.2 0.0 all-gather.3.cloned.1.call-start
  370.2 0.5 all-gather.3.cloned.1.call-update
  371.4 0.0 copy-done.3
  371.5 14.2 %all_gather.9.rhs = f32[1024,128]{1,0:T(8,128)} all-gather(f32[256,128]{1,0:T(8,128)S(1)} %add.77), channel_id=1, replica_groups=mesh['x'=4,'z'=16,'core'=2,'chain'=4] {'chain'}, dimensions={0}, use_global_device_ids=true | all-gather | bytes 655360 | tf_op jit(solution)/shard_map/all_gather | solution.py:216
  385.6 12.1 %all-gather.5.cloned.1.call-done.inverse = f32[1024,256]{1,0:T(8,128)} async-done(((f32[256,256]{1,0:T(8,128)}), f32[1024,256]{1,0:T(8,128)}) %all-gather.5.cloned.1.call-update) | async-done | bytes 1048592 | tf_op jit(solution)/shard_map/all_gather | solution.py:215
  397.7 36.5 %all-gather.3.cloned.1.call-done.lower = bf16[1024,768]{1,0:T(8,128)(2,1)} async-done(((bf16[256,768]{1,0:T(8,128)(2,1)}), bf16[1024,768]{1,0:T(8,128)(2,1)}) %all-gather.3.cloned.1.call-update) | async-done | bytes 1572880 | tf_op jit(solution)/shard_map/all_gather | solution.py:214
  434.2 6.4 %solve.1 = (f32[256,128]{1,0:T(8,128)}, f32[512,128]{1,0:T(8,128)}) custom-call(s32[1]{0:T(128)} %bitcast.7.spot, s32[1]{0:T(128)S(6)} %copy.38.pivots, f32[1024,128]{1,0:T(8,128)} %all_gather.9.rhs, bf16[1024,768]{1,0:T(8,128)(2,1)} %all-gather.3.cloned.1.call-done.lower, f32[1024,256]{1,0:T(8,128)} %all-gather.5.cloned.1.call-done.inverse, ...), custom_call_target="tpu_custom_call" | custom-call | tf_op jit(solution)/shard_map/solve/pallas_call | solution.py:184
  (1 shorter events, 0.0 us)
Async XLA Ops:
  8.0 359.1 %reduce-scatter.5.cloned.1.call-start = ((), (), s32[]{:S(2)}) async-start(), calls=%async_computation.6 | async-start | bytes 6684672 | tf_op jit(solution)/shard_map/reduce_scatter | solution.py:206
  226.1 4.4 copy-start.1
  231.2 135.9 %copy-start = (s32[88]{0:T(128)S(1)}, s32[88]{0:T(128)}, u32[]{:S(2)}) copy-start(s32[88]{0:T(128)} %place.1) | copy-start | bytes 1060
  231.2 135.9 %copy-start.2 = (bf16[88,128,128]{2,1,0:T(8,128)(2,1)S(1)}, bf16[88,128,128]{2,1,0:T(8,128)(2,1)}, u32[]{:S(2)}) copy-start(bf16[88,128,128]{2,1,0:T(8,128)(2,1)} %blocks.1) | copy-start | bytes 8650756
  231.2 135.9 %copy-start.4 = (s32[88,1]{0,1:T(1,128)S(1)}, s32[88,1]{0,1:T(1,128)}, u32[]{:S(2)}) copy-start(s32[88,1]{0,1:T(1,128)} %param.12) | copy-start | bytes 1060
  367.1 4.3 copy-start.3
  369.6 28.1 %all-gather.5.cloned.1.call-start = ((), (), s32[]{:S(2)}) async-start(), calls=%async_computation.8 | async-start | bytes 1310720 | tf_op jit(solution)/shard_map/all_gather | solution.py:215
  370.2 64.0 %all-gather.3.cloned.1.call-start = ((), (), s32[]{:S(2)}) async-start(), calls=%async_computation.7 | async-start | bytes 1966080 | tf_op jit(solution)/shard_map/all_gather | solution.py:214
Sparse Core Ops, SparseCore 0:
  253.0 95.3 reduce-scatter.4
Sparse Core Ops, SparseCore 1:
  372.2 25.5 all-gather.4
  399.7 34.4 all-gather.2

commit v2 on v1

--- a/solution.py
+++ b/solution.py
@@ -13,6 +13,9 @@
 PEERS = 32
 LABEL_ROWS = 16
 OWNED = 6
+COUNT_LANE = 126
+OVER_LANE = 127
+CHUNK = OWNED * BR + 8
 
 
 def slot_table(blocks, fronts, places, dest_count, slot_width):
@@ -45,7 +48,7 @@
     return lax.psum_scatter(merged, "chain", scatter_dimension=0, tiled=True)
 
 
-def send_kernel(front, place, blocks, out, over, marks, tags, counts, sem, tag_sem):
+def send_kernel(front, place, blocks, out, marks, tags, counts, sem, tag_sem):
     for peer in range(PEERS):
         counts[peer] = 0
     marks[...] = jnp.full(marks.shape, -1.0, jnp.float32)
@@ -78,10 +81,11 @@
         )
 
     missed, sent = lax.fori_loop(0, front.shape[0], step, (jnp.int32(0), jnp.int32(0)))
-    over[0] = missed
-    half = marks[...].astype(jnp.bfloat16)
-    tags[:, 0:8, :] = half
-    tags[:, 8:16, :] = half
+    for peer in range(PEERS):
+        row = jnp.where(lane == COUNT_LANE, counts[peer].astype(jnp.float32), marks[peer])
+        row = jnp.where(lane == OVER_LANE, missed.astype(jnp.float32), row)
+        tags[peer, 0:8, :] = row.astype(jnp.bfloat16)
+        tags[peer, 8:16, :] = row.astype(jnp.bfloat16)
     tag_copy = pltpu.make_async_copy(tags, out.at[:, pl.ds(SLOTS * BR, LABEL_ROWS)], tag_sem)
     tag_copy.start()
 
@@ -96,16 +100,13 @@
 def pack(fronts, places, blocks):
     return pl.pallas_call(
         send_kernel,
-        out_shape=(
-            jax.ShapeDtypeStruct((PEERS, SLOTS * BR + LABEL_ROWS, 128), jnp.bfloat16),
-            jax.ShapeDtypeStruct((1,), jnp.int32),
-        ),
+        out_shape=jax.ShapeDtypeStruct((PEERS, SLOTS * BR + LABEL_ROWS, 128), jnp.bfloat16),
         in_specs=[
             pl.BlockSpec(memory_space=pltpu.SMEM),
             pl.BlockSpec(memory_space=pltpu.SMEM),
-            pl.BlockSpec(memory_space=pl.ANY),
-        ],
-        out_specs=(pl.BlockSpec(memory_space=pl.ANY), pl.BlockSpec(memory_space=pltpu.SMEM)),
+            pl.BlockSpec(memory_space=pltpu.VMEM),
+        ],
+        out_specs=pl.BlockSpec(memory_space=pl.ANY),
         scratch_shapes=[
             pltpu.VMEM((PEERS, 8, 128), jnp.float32),
             pltpu.VMEM((PEERS, LABEL_ROWS, 128), jnp.bfloat16),
@@ -117,51 +118,86 @@
     )(fronts, places, blocks)
 
 
-def gather_kernel(index, block, out):
-    source = pl.program_id(0)
-
-    @pl.when(source == 0)
-    def _():
-        out[...] = jnp.zeros(out.shape, jnp.float32)
-
-    for slot in range(SLOTS):
-        target = index[source * SLOTS + slot]
-
-        @pl.when(target >= 0)
-        def _():
-            out[target] += block[0, slot * BR : (slot + 1) * BR, :].astype(jnp.float32)
+def gather_kernel(index, received, out, total, landed, sems, sem):
+    def fetch(i, at):
+        def slot(j, spot):
+            pltpu.make_async_copy(
+                received.at[i, pl.ds(pl.multiple_of(j * BR, BR), BR)], landed.at[spot], sems.at[i]
+            ).start()
+            return spot + 1
+
+        return lax.fori_loop(0, index[i, 0, COUNT_LANE], slot, at)
+
+    lax.fori_loop(0, PEERS, fetch, jnp.int32(0))
+    total[...] = jnp.zeros(total.shape, jnp.float32)
+
+    def source(i, carry):
+        missed, at = carry
+        count = index[i, 0, COUNT_LANE]
+
+        def arrive(j, carry):
+            pltpu.make_async_copy(received.at[0, pl.ds(0, BR)], landed.at[0], sems.at[i]).wait()
+            return carry
+
+        lax.fori_loop(0, count, arrive, 0)
+
+        def slot(j, spot):
+            target = index[i, 0, j]
+            chunk = target // OWNED
+            start = pl.multiple_of((target - chunk * OWNED) * BR, BR)
+            total[chunk, pl.ds(start, BR), :] += landed[spot].astype(jnp.float32)
+            return spot + 1
+
+        at = lax.fori_loop(0, count, slot, at)
+        return missed + index[i, 0, OVER_LANE], at
+
+    missed, _ = lax.fori_loop(0, PEERS, source, (jnp.int32(0), jnp.int32(0)))
+    total[:, OWNED * BR :, :] = jnp.full((16, 8, 128), missed.astype(jnp.float32))
+    copy = pltpu.make_async_copy(total, out, sem)
+    copy.start()
+    copy.wait()
 
 
 def add_up(index, received):
-    rows = received.shape[1]
     return pl.pallas_call(
         gather_kernel,
-        out_shape=jax.ShapeDtypeStruct((16 * OWNED, BR, 128), jnp.float32),
-        grid_spec=pltpu.PrefetchScalarGridSpec(
-            num_scalar_prefetch=1,
-            grid=(PEERS,),
-            in_specs=[pl.BlockSpec((1, rows, 128), lambda i, ids: (i, 0, 0))],
-            out_specs=pl.BlockSpec((16 * OWNED, BR, 128), lambda i, ids: (0, 0, 0)),
-        ),
+        out_shape=jax.ShapeDtypeStruct((16, CHUNK, 128), jnp.float32),
+        in_specs=[
+            pl.BlockSpec(memory_space=pltpu.SMEM),
+            pl.BlockSpec(memory_space=pl.ANY),
+        ],
+        out_specs=pl.BlockSpec(memory_space=pl.ANY),
+        scratch_shapes=[
+            pltpu.VMEM((16, CHUNK, 128), jnp.float32),
+            pltpu.VMEM((PEERS * SLOTS, BR, 128), jnp.bfloat16),
+            pltpu.SemaphoreType.DMA((PEERS,)),
+            pltpu.SemaphoreType.DMA,
+        ],
         name="add_up",
     )(index, received)
 
 
-def solve_kernel(spot, pivots, rhs, lower, inverse, owned, update, solved_out, update_out, kept):
+def solve_kernel(spot, pivots, rhs, *refs):
+    lowers, inverses = refs[0:4], refs[4:8]
+    owned, update, solved_out, update_out, lower, inverse, kept = refs[8:]
     chain_at = spot[0]
     live_count = pivots[0]
+    for shift in range(4):
+        block = (chain_at - shift) & 3
+        lower[block] = lowers[shift][...]
+        inverse[block] = inverses[shift][...]
     for block in range(4):
         rows = slice(block * 256, (block + 1) * 256)
         partial = rhs[rows, :]
         if block > 0:
             partial = partial - jnp.dot(
-                lower[rows, 0 : block * 256],
+                lower[block, :, 0 : block * 256],
                 kept[0 : block * 256, :],
                 preferred_element_type=jnp.float32,
             )
         row = block * 256 + lax.broadcasted_iota(jnp.int32, (256, 128), 0)
         product = jnp.dot(
-            inverse[rows, :],
+            inverse[block],
             partial,
             precision=lax.Precision.HIGHEST,
             preferred_element_type=jnp.float32,
@@ -178,7 +214,7 @@
     )
 
 
-def solve(spot, pivots, rhs, lower, inverse, owned, update):
+def solve(spot, pivots, rhs, lowers, inverses, owned, update):
     smem = pl.BlockSpec(memory_space=pltpu.SMEM)
     vmem = pl.BlockSpec(memory_space=pltpu.VMEM)
     return pl.pallas_call(
@@ -187,35 +223,48 @@
             jax.ShapeDtypeStruct((256, 128), jnp.float32),
             jax.ShapeDtypeStruct((512, 128), jnp.float32),
         ),
-        in_specs=[smem, smem, vmem, vmem, vmem, vmem, vmem],
+        in_specs=[smem, smem] + [vmem] * 11,
         out_specs=(vmem, vmem),
-        scratch_shapes=[pltpu.VMEM((1024, 128), jnp.bfloat16)],
+        scratch_shapes=[
+            pltpu.VMEM((4, 256, 768), jnp.bfloat16),
+            pltpu.VMEM((4, 256, 256), jnp.float32),
+            pltpu.VMEM((1024, 128), jnp.bfloat16),
+        ],
         name="solve",
-    )(spot, pivots, rhs, lower, inverse, owned, update)
+    )(spot, pivots, rhs, *lowers, *inverses, owned, update)
+
+
+def around_chain(value):
+    moved = [
+        lax.ppermute(value, "chain", [(i, (i + shift) % 4) for i in range(4)])
+        for shift in (1, 2, 3)
+    ]
+    return (value, *moved)
 
 
 def body(
     rhs, child_blocks, dest_front, dest_place, front_pivots, diag_inv, lower_factor, update_factor
 ):
     fronts = dest_front.reshape(-1)
-    packed, over = pack(fronts, dest_place, child_blocks)
-    overflow = lax.pmax(over, ALL)
+    packed = pack(fronts, dest_place, child_blocks)
     received = lax.all_to_all(packed, SLAB, split_axis=0, concat_axis=0, tiled=True)
-    index = received[:, SLOTS * BR, :SLOTS].astype(jnp.int32).reshape(-1)
+    index = received[:, SLOTS * BR : SLOTS * BR + 1, :].astype(jnp.int32)
     dense = add_up(index, received)
-    owned = lax.psum_scatter(dense, "z", scatter_dimension=0, tiled=True)
-    owned = lax.cond(
-        overflow[0] > 0,
-        lambda fast: full_exchange(child_blocks, fronts, dest_place),
-        lambda fast: fast,
-        owned,
-    )
-    owned = owned.reshape(OWNED * BR, 128)
-    all_lower = lax.all_gather(lower_factor, "chain", axis=0, tiled=True)
-    all_inverse = lax.all_gather(diag_inv, "chain", axis=0, tiled=True)
-    all_rhs = lax.all_gather(rhs + owned[:256], "chain", axis=0, tiled=True)
+    dense, lower_factor, diag_inv = lax.optimization_barrier((dense, lower_factor, diag_inv))
+    owned = lax.psum_scatter(dense, "z", scatter_dimension=0, tiled=True).reshape(CHUNK, 128)
+    lowers = around_chain(lower_factor)
+    inverses = around_chain(diag_inv)
     spot = lax.axis_index("chain").astype(jnp.int32).reshape(1)
-    return solve(spot, front_pivots, all_rhs, all_lower, all_inverse, owned, update_factor)
+
+    def finish(mine):
+        all_rhs = lax.all_gather(rhs + mine[:256], "chain", axis=0, tiled=True)
+        return solve(spot, front_pivots, all_rhs, lowers, inverses, mine, update_factor)
+
+    def general(mine):
+        exchanged = full_exchange(child_blocks, fronts, dest_place)
+        return finish(jnp.concatenate([exchanged.reshape(OWNED * BR, 128), mine[OWNED * BR :]]))
+
+    return lax.cond(owned[OWNED * BR, 0] > 0, general, finish, owned)
 
 
 def solution(mesh):

time: 450 us -> 286 us (0.64)
  blocking collectives: 269 us -> 153 us
  Pallas kernels: 105 us -> 19.6 us
  starting transfers between devices: 0.08 us -> 20.9 us
  waiting for transfers between devices: 49.7 us -> 69.1 us
    pmax x1 -> x0, blocking collectives: 114 us -> none  [body(): overflow = lax.pmax(over, ALL)]
    pallas_call x2, Pallas kernels: 98.4 us -> 12.5 us  [the longest x1 7.69 us: add_up(): pl.pallas_call(gather_kernel, out_shape=jax.ShapeDtypeStruct((16, CHUNK,...]
    unnamed x3 -> x2, waiting for transfers between devices: 1.1 us -> 69.1 us
    all_gather x2 -> x0, waiting for transfers between devices: 48.6 us -> none  [the longest x1 36.5 us: body(): all_lower = lax.all_gather(lower_factor, 'chain', axis=0, tiled=True)]
    ppermute x0 -> x6, starting transfers between devices: none -> 20.8 us  [around_chain(): lax.ppermute(value, 'chain', [(i, (i + shift) % 4) for i in range(4)])]
  transfers between devices with their start and end apart: 3 -> 7, of which waited for: 2 -> 1; matrix products, arithmetic and copies ran while one was open for 0% -> 0% of each run, Pallas kernels for 0% -> 0%
where the time goes in v2:
time: 286 us
  blocking collectives  153 us (53%)
  waiting for transfers between devices  69.1 us (24%)
  starting transfers between devices  20.9 us (7%)
  Pallas kernels  19.6 us (7%)
  between operations  14.9 us (5%)
  local copies, waits for them, and re-layouts  6.28 us (2%)
    all_to_all x1, blocking collectives, body(): lax.all_to_all(packed, SLAB, split_axis=0, concat_axis=0, tiled=True)  139 us
    unnamed x2, waiting for transfers between devices  69.1 us
    ppermute x6, starting transfers between devices, around_chain(): lax.ppermute(value, 'chain', [(i, (i + shift) % 4) for i in range(4)])  20.8 us
    all_gather x1, blocking collectives, finish(): all_rhs = lax.all_gather(rhs + mine[:256], 'chain', axis=0, tiled=True)  14 us
    pallas_call x1, Pallas kernels, add_up(): pl.pallas_call(gather_kernel, out_shape=jax.ShapeDtypeStruct((16, CHUNK,...  7.69 us
    pallas_call x1, Pallas kernels, solve(): pl.pallas_call(solve_kernel, out_shape=(jax.ShapeDtypeStruct((256, 128),...  7.16 us
  transfers between devices with their start and end apart: 7, of which 1 were waited for; matrix products, arithmetic and copies ran while one was open for 0% of the time, Pallas kernels for 0%

profile of v2, /device:TPU:6, one launch (start us, length us, event | category | flops | bytes accessed | tf_op | source)
XLA Modules:
  0.0 285.6 jit_solution(9953769215343343761)
XLA Ops:
  7.2 0.0 reduce-scatter.7.cloned.1.call-start
  7.2 4.8 %pack.1 = bf16[32,1424,128]{2,1,0:T(8,128)(2,1)} custom-call(s32[88]{0:T(128)} %bitcast.23, s32[88]{0:T(128)} %place.1, bf16[88,128,128]{2,1,0:T(8,128)(2,1)} %blocks.1), custom_call_target="tpu_custom_call" | custom-call | tf_op jit(solution)/shard_map/pack/pallas_call | solution.py:101
  12.0 139.2 %all_to_all.14.received = bf16[32,1424,128]{2,1,0:T(8,128)(2,1)S(1)} all-to-all(bf16[32,1424,128]{2,1,0:T(8,128)(2,1)} %pack.1), channel_id=1, replica_groups=mesh['x'=4,'z'=16,'core'=2,'chain'=4] {'x','core','chain'}, dimensions={0} | all-to-all | bytes 23330816 | tf_op jit(solution)/shard_map/all_to_all | solution.py:250
  151.3 4.4 %copy-done.1 = bf16[32,1424,128]{2,1,0:T(8,128)(2,1)} copy-done((bf16[32,1424,128]{2,1,0:T(8,128)(2,1)}, bf16[32,1424,128]{2,1,0:T(8,128)(2,1)S(1)}, u32[]{:S(2)}) %copy-start.1) | copy-done | bytes 11665432
  155.6 0.6 slice_convert_fusion.index
  156.2 0.0 copy-start.9
  156.3 7.7 %add_up.1 = f32[16,776,128]{2,1,0:T(8,128)} custom-call(s32[32,1,128]{2,1,0:T(1,128)} %slice_convert_fusion.index, bf16[32,1424,128]{2,1,0:T(8,128)(2,1)} %copy-done.1), custom_call_target="tpu_custom_call" | custom-call | tf_op jit(solution)/shard_map/add_up/pallas_call | solution.py:162
  164.0 0.0 reduce-scatter.7.cloned.1.call-update
  164.0 0.0 copy-done.5
  164.0 2.2 collective-permute-start.3
  166.1 0.0 copy-done.4
  166.2 3.4 %collective-permute-start = (bf16[256,768]{1,0:T(8,128)(2,1)S(1)}, bf16[256,768]{1,0:T(8,128)(2,1)}, u32[]{:S(2)}, u32[]{:S(2)}) collective-permute-start(bf16[256,768]{1,0:T(8,128)(2,1)S(1)} %copy-done.4), channel_id=1, source_target_pairs={{0,1},{1,2},{2,3},{3,0},{4,5},{5,6},{6,7},{7,4},{8,9},{9,10},{10,1... | collective-permute-start | bytes 1179656 | tf_op jit(solution)/shard_map/ppermute | solution.py:239
  169.6 4.9 %collective-permute-start.1 = (bf16[256,768]{1,0:T(8,128)(2,1)S(1)}, bf16[256,768]{1,0:T(8,128)(2,1)}, u32[]{:S(2)}, u32[]{:S(2)}) collective-permute-start(bf16[256,768]{1,0:T(8,128)(2,1)S(1)} %copy-done.4), channel_id=1, source_target_pairs={{0,2},{1,3},{2,0},{3,1},{4,6},{5,7},{6,4},{7,5},{8,10},{9,11},{10,... | collective-permute-start | bytes 1179656 | tf_op jit(solution)/shard_map/ppermute | solution.py:239
  174.4 2.6 collective-permute-start.2
  177.1 2.9 %collective-permute-start.4 = (f32[256,256]{1,0:T(8,128)S(1)}, f32[256,256]{1,0:T(8,128)}, u32[]{:S(2)}, u32[]{:S(2)}) collective-permute-start(f32[256,256]{1,0:T(8,128)S(1)} %copy-done.5), channel_id=1, source_target_pairs={{0,2},{1,3},{2,0},{3,1},{4,6},{5,7},{6,4},{7,5},{8,10},{9,11},{10,... | collective-permute-start | bytes 786440 | tf_op jit(solution)/shard_map/ppermute | solution.py:239
  180.0 0.0 collective-permute-done.3
  180.0 0.7 copy-done.6
  180.7 4.9 %collective-permute-start.5 = (f32[256,256]{1,0:T(8,128)S(1)}, f32[256,256]{1,0:T(8,128)}, u32[]{:S(2)}, u32[]{:S(2)}) collective-permute-start(f32[256,256]{1,0:T(8,128)S(1)} %copy-done.5), channel_id=1, source_target_pairs={{0,3},{1,0},{2,1},{3,2},{4,7},{5,4},{6,5},{7,6},{8,11},{9,8},{10,9... | collective-permute-start | bytes 786440 | tf_op jit(solution)/shard_map/ppermute | solution.py:239
  185.6 69.1 %reduce-scatter.7.cloned.1.call-done = f32[1,776,128]{2,1,0:T(8,128)} async-done(((f32[16,776,128]{2,1,0:T(8,128)}), f32[1,776,128]{2,1,0:T(8,128)}) %reduce-scatter.7.cloned.1.call-update) | async-done | bytes 397328
  254.7 1.2 slice.26
  256.5 0.0 collective-permute-done.4
  256.5 0.0 collective-permute-done.5
  256.5 0.0 collective-permute-done
  256.6 0.0 collective-permute-done.1
  256.6 0.0 collective-permute-done.2
  256.6 0.0 copy-done
  256.6 0.0 copy-done.2
  256.6 0.0 copy-done.9
  256.6 22.1 %conditional.1 = ((f32[256,128]{1,0:T(8,128)}, f32[512,128]{1,0:T(8,128)})) conditional(s32[]{:T(128)} %bitcast.9, (f32[776,128]{1,0:T(8,128)}, f32[256,128]{1,0:T(8,128)}, s32[1]{0:T(128)}, s32[1]{0:T(128)}, bf16[256,768]{1,0:T(8,128)(2,1)S(1)}, /*index=5*/bf16[256,768]{1,0:T(8,128)(2,1)}, bf16[256,768]{1,0:T(8,128)(2,1)}, ...), branch_computations={%region_1.0_spmd, %region_2.6_spmd} | conditional | flops 205713824 | bytes 119320864 | solution.py:267
  256.6 1.0 slice_add_fusion
  257.6 14.0 %all_gather.4.rhs = f32[1024,128]{1,0:T(8,128)} all-gather(f32[256,128]{1,0:T(8,128)S(1)} %slice_add_fusion), channel_id=1, replica_groups=mesh['x'=4,'z'=16,'core'=2,'chain'=4] {'chain'}, dimensions={0}, use_global_device_ids=true | all-gather | bytes 655360 | tf_op jit(solution)/shard_map/cond/branch_0_fun/all_gather | solution.py:260
  271.6 7.2 %solve.2 = (f32[256,128]{1,0:T(8,128)}, f32[512,128]{1,0:T(8,128)}) custom-call(s32[1]{0:T(128)} %get-tuple-element.60.spot, s32[1]{0:T(128)} %get-tuple-element.61.pivots, f32[1024,128]{1,0:T(8,128)} %all_gather.4.rhs, bf16[256,768]{1,0:T(8,128)(2,1)S(1)} %get-tuple-element.64.refs_0_, bf16[256,768]{1,0:T(8,128)(2,1)} %get-tuple-element.65.refs_1_, ...), custom_call_target="tpu_custom_call" | custom-call | tf_op jit(solution)/shard_map/cond/branch_0_fun/solve/pallas_call | solution.py:220
  (6 shorter events, 0.0 us)
Async XLA Ops:
  7.2 247.5 %reduce-scatter.7.cloned.1.call-start = ((), (), s32[]{:S(2)}) async-start(), calls=%async_computation.6 | async-start | bytes 6754304
  151.3 4.4 %copy-start.1 = (bf16[32,1424,128]{2,1,0:T(8,128)(2,1)}, bf16[32,1424,128]{2,1,0:T(8,128)(2,1)S(1)}, u32[]{:S(2)}) copy-start(bf16[32,1424,128]{2,1,0:T(8,128)(2,1)S(1)} %all_to_all.14.received) | copy-start | bytes 34996228
  156.2 7.7 %copy-start.5 = (f32[256,256]{1,0:T(8,128)S(1)}, f32[256,256]{1,0:T(8,128)}, u32[]{:S(2)}) copy-start(f32[256,256]{1,0:T(8,128)} %param.15) | copy-start | bytes 786436
  156.2 9.9 %copy-start.4 = (bf16[256,768]{1,0:T(8,128)(2,1)S(1)}, bf16[256,768]{1,0:T(8,128)(2,1)}, u32[]{:S(2)}) copy-start(bf16[256,768]{1,0:T(8,128)(2,1)} %param.16) | copy-start | bytes 1179652
  156.2 100.3 %copy-start = (s32[88]{0:T(128)S(1)}, s32[88]{0:T(128)}, u32[]{:S(2)}) copy-start(s32[88]{0:T(128)} %place.1) | copy-start | bytes 1060
  156.2 100.4 %copy-start.2 = (bf16[88,128,128]{2,1,0:T(8,128)(2,1)S(1)}, bf16[88,128,128]{2,1,0:T(8,128)(2,1)}, u32[]{:S(2)}) copy-start(bf16[88,128,128]{2,1,0:T(8,128)(2,1)} %blocks.1) | copy-start | bytes 8650756
  156.2 100.4 %copy-start.9 = (s32[88,1]{0,1:T(1,128)S(1)}, s32[88,1]{0,1:T(1,128)}, u32[]{:S(2)}) copy-start(s32[88,1]{0,1:T(1,128)} %param.12) | copy-start | bytes 1060
  164.0 16.0 %collective-permute-start.3 = (f32[256,256]{1,0:T(8,128)S(1)}, f32[256,256]{1,0:T(8,128)S(1)}, u32[]{:S(2)}, u32[]{:S(2)}) collective-permute-start(f32[256,256]{1,0:T(8,128)S(1)} %copy-done.5), channel_id=1, source_target_pairs={{0,1},{1,2},{2,3},{3,0},{4,5},{5,6},{6,7},{7,4},{8,9},{9,10},{10,1... | collective-permute-start | bytes 786440 | tf_op jit(solution)/shard_map/ppermute | solution.py:239
  166.2 90.4 %collective-permute-start = (bf16[256,768]{1,0:T(8,128)(2,1)S(1)}, bf16[256,768]{1,0:T(8,128)(2,1)}, u32[]{:S(2)}, u32[]{:S(2)}) collective-permute-start(bf16[256,768]{1,0:T(8,128)(2,1)S(1)} %copy-done.4), channel_id=1, source_target_pairs={{0,1},{1,2},{2,3},{3,0},{4,5},{5,6},{6,7},{7,4},{8,9},{9,10},{10,1... | collective-permute-start | bytes 1179656 | tf_op jit(solution)/shard_map/ppermute | solution.py:239
  169.6 87.0 %collective-permute-start.1 = (bf16[256,768]{1,0:T(8,128)(2,1)S(1)}, bf16[256,768]{1,0:T(8,128)(2,1)}, u32[]{:S(2)}, u32[]{:S(2)}) collective-permute-start(bf16[256,768]{1,0:T(8,128)(2,1)S(1)} %copy-done.4), channel_id=1, source_target_pairs={{0,2},{1,3},{2,0},{3,1},{4,6},{5,7},{6,4},{7,5},{8,10},{9,11},{10,... | collective-permute-start | bytes 1179656 | tf_op jit(solution)/shard_map/ppermute | solution.py:239
  174.4 82.1 %collective-permute-start.2 = (bf16[256,768]{1,0:T(8,128)(2,1)S(1)}, bf16[256,768]{1,0:T(8,128)(2,1)}, u32[]{:S(2)}, u32[]{:S(2)}) collective-permute-start(bf16[256,768]{1,0:T(8,128)(2,1)S(1)} %copy-done.4), channel_id=1, source_target_pairs={{0,3},{1,0},{2,1},{3,2},{4,7},{5,4},{6,5},{7,6},{8,11},{9,8},{10,9... | collective-permute-start | bytes 1179656 | tf_op jit(solution)/shard_map/ppermute | solution.py:239
  177.1 79.4 %collective-permute-start.4 = (f32[256,256]{1,0:T(8,128)S(1)}, f32[256,256]{1,0:T(8,128)}, u32[]{:S(2)}, u32[]{:S(2)}) collective-permute-start(f32[256,256]{1,0:T(8,128)S(1)} %copy-done.5), channel_id=1, source_target_pairs={{0,2},{1,3},{2,0},{3,1},{4,6},{5,7},{6,4},{7,5},{8,10},{9,11},{10,... | collective-permute-start | bytes 786440 | tf_op jit(solution)/shard_map/ppermute | solution.py:239
  180.0 0.7 copy-start.6
  180.7 75.8 %collective-permute-start.5 = (f32[256,256]{1,0:T(8,128)S(1)}, f32[256,256]{1,0:T(8,128)}, u32[]{:S(2)}, u32[]{:S(2)}) collective-permute-start(f32[256,256]{1,0:T(8,128)S(1)} %copy-done.5), channel_id=1, source_target_pairs={{0,3},{1,0},{2,1},{3,2},{4,7},{5,4},{6,5},{7,6},{8,11},{9,8},{10,9... | collective-permute-start | bytes 786440 | tf_op jit(solution)/shard_map/ppermute | solution.py:239
Sparse Core Ops, SparseCore 0:
  164.1 90.5 reduce-scatter.6

commit v3 on v2

v3 whole, which is shorter than its diff:
```python
import jax
import jax.numpy as jnp
from jax import lax
from jax.experimental import pallas as pl
from jax.experimental.pallas import tpu as pltpu
from jax.sharding import Mesh, PartitionSpec as P

BR = 128
FRONT = ("x", "z", "core")
ALL = ("x", "z", "core", "chain")
SLAB = ("x", "core", "chain")
LINE = ("x", "core")
SLOTS = 5
HOPS = 6
PEERS = 32
GROUPS = 8
LABEL_ROWS = 16
OWNED = 6
HOP_LANE = 64
STRAY_LANE = 125
COUNT_LANE = 126
OVER_LANE = 127
PIVOT_ROWS = 256
FLAG_ROWS = 8
CHUNK = OWNED * BR + FLAG_ROWS


def slot_table(blocks, fronts, places, dest_count, slot_width):
    block_count = fronts.shape[0]
    sequence = jnp.arange(block_count, dtype=jnp.int32)
    earlier = (fronts[None, :] == fronts[:, None]) & (sequence[None, :] < sequence[:, None])
    rank_of = jnp.sum(earlier.astype(jnp.int32), axis=1)
    target = fronts * slot_width + rank_of
    source = jnp.full((dest_count * slot_width,), block_count, jnp.int32).at[target].set(sequence)
    slot_data = jnp.take(blocks, source, axis=0, mode="fill", fill_value=0)
    labels = jnp.take(places, source, axis=0, mode="fill", fill_value=-1)
    return (
        slot_data.reshape((dest_count, slot_width) + blocks.shape[1:]),
        labels.reshape(dest_count, slot_width),
    )


def full_exchange(child_blocks, fronts, places):
    slot_data, labels = slot_table(child_blocks, fronts, places, 128, 2)
    received = lax.all_to_all(slot_data, FRONT, split_axis=0, concat_axis=0, tiled=True)
    tags = lax.all_to_all(labels, FRONT, split_axis=0, concat_axis=0, tiled=True).reshape(-1)
    placed = jnp.where(
        tags < 8, tags // 2 * OWNED + tags % 2, (tags - 8) // 4 * OWNED + 2 + (tags - 8) % 4
    )
    placed = jnp.where(tags < 0, -1, placed)
    row_ids = jnp.arange(4 * OWNED, dtype=jnp.int32)
    onehot = (placed[None, :] == row_ids[:, None]).astype(jnp.bfloat16)
    flattened = received.reshape((-1,) + received.shape[2:])
    merged = jnp.einsum("km,mrs->krs", onehot, flattened, preferred_element_type=jnp.float32)
    return lax.psum_scatter(merged, "chain", scatter_dimension=0, tiled=True)


def write_tags(marks, tags, counts, strays, missed, count):
    lane = lax.broadcasted_iota(jnp.int32, (8, 128), 1)
    for peer in range(count):
        row = jnp.where(lane == COUNT_LANE, counts[peer].astype(jnp.float32), marks[peer])
        if strays is not None:
            row = jnp.where(lane == STRAY_LANE, strays[peer].astype(jnp.float32), row)
        row = jnp.where(lane == OVER_LANE, missed.astype(jnp.float32), row)
        tags[peer, 0:8, :] = row.astype(jnp.bfloat16)
        tags[peer, 8:16, :] = row.astype(jnp.bfloat16)


def send_kernel(spot, front, place, blocks, out, marks, tags, counts, strays, late, sem, tag_sem):
    for peer in range(PEERS):
        counts[peer] = 0
        strays[peer] = 0
    marks[...] = jnp.full(marks.shape, -1.0, jnp.float32)
    lane = lax.broadcasted_iota(jnp.int32, (8, 128), 1)

    def route(i):
        where_front = front[i]
        target = place[i]
        pivot = target < 8
        owner = jnp.where(pivot, target >> 1, (target - 8) >> 2)
        peer = ((where_front >> 5) * 2 + (where_front & 1)) * 4 + owner
        index = ((where_front >> 1) & 15) * OWNED + jnp.where(
            pivot, target & 1, 2 + ((target - 8) & 3)
        )
        live = target >= 0
        return live, jnp.where(live, peer, 0), index

    def launch(i, peer, used):
        pltpu.make_async_copy(
            blocks.at[i], out.at[peer, pl.ds(pl.multiple_of(used * BR, BR), BR)], sem
        ).start()

    def direct(i, carry):
        left, sent = carry
        live, peer, index = route(i)
        used = counts[peer]
        fits = live & (used < SLOTS)

        @pl.when(fits)
        def _():
            counts[peer] = used + 1
            launch(i, peer, used)
            marks[peer] = jnp.where(lane == used, index.astype(jnp.float32), marks[peer])

        @pl.when(live & (used >= SLOTS))
        def _():
            late[left] = i

        return (
            left + jnp.where(live & (used >= SLOTS), 1, 0),
            sent + jnp.where(fits, 1, 0),
        )

    left, sent = lax.fori_loop(0, front.shape[0], direct, (jnp.int32(0), jnp.int32(0)))

    def detour(k, carry):
        missed, sent = carry
        i = late[k]
        _, home, index = route(i)
        group = home >> 2
        chosen = jnp.int32(-1)
        for h in reversed(range(GROUPS - 1)):
            turn = lax.rem(spot[0] + k + h, GROUPS - 1)
            peer = (((group + 1 + turn) & 7) << 2) + (home & 3)
            chosen = jnp.where(counts[peer] < SLOTS, peer, chosen)
        fits = chosen >= 0

        @pl.when(fits)
        def _():
            used = counts[chosen]
            counts[chosen] = used + 1
            strays[chosen] = strays[chosen] + 1
            launch(i, chosen, used)
            row = jnp.where(lane == used, index.astype(jnp.float32), marks[chosen])
            marks[chosen] = jnp.where(lane == HOP_LANE + used, group.astype(jnp.float32), row)

        return missed + jnp.where(fits, 0, 1), sent + jnp.where(fits, 1, 0)

    missed, sent = lax.fori_loop(0, left, detour, (jnp.int32(0), sent))
    write_tags(marks, tags, counts, strays, missed, PEERS)
    tag_copy = pltpu.make_async_copy(tags, out.at[:, pl.ds(SLOTS * BR, LABEL_ROWS)], tag_sem)
    tag_copy.start()

    def drain(i, carry):
        pltpu.make_async_copy(blocks.at[0], out.at[0, pl.ds(0, BR)], sem).wait()
        return carry

    lax.fori_loop(0, sent, drain, 0)
    tag_copy.wait()


def pack(turn, fronts, places, blocks):
    smem = pl.BlockSpec(memory_space=pltpu.SMEM)
    return pl.pallas_call(
        send_kernel,
        out_shape=jax.ShapeDtypeStruct((PEERS, SLOTS * BR + LABEL_ROWS, 128), jnp.bfloat16),
        in_specs=[smem, smem, smem, pl.BlockSpec(memory_space=pltpu.VMEM)],
        out_specs=pl.BlockSpec(memory_space=pl.ANY),
        scratch_shapes=[
            pltpu.VMEM((PEERS, 8, 128), jnp.float32),
            pltpu.VMEM((PEERS, LABEL_ROWS, 128), jnp.bfloat16),
            pltpu.SMEM((PEERS,), jnp.int32),
            pltpu.SMEM((PEERS,), jnp.int32),
            pltpu.SMEM((128,), jnp.int32),
            pltpu.SemaphoreType.DMA,
            pltpu.SemaphoreType.DMA,
        ],
        compiler_params=pltpu.CompilerParams(vmem_limit_bytes=8 << 20),
        name="pack",
    )(turn, fronts, places, blocks)


def forward_kernel(index, received, out, marks, tags, counts, sem, tag_sem):
    for peer in range(GROUPS):
        counts[peer] = 0
    marks[...] = jnp.full(marks.shape, -1.0, jnp.float32)
    lane = lax.broadcasted_iota(jnp.int32, (8, 128), 1)

    def source(i, carry):
        def slot(j, carry):
            missed, sent = carry
            home = index[i, 0, HOP_LANE + j]
            stray = home >= 0
            used = counts[jnp.maximum(home, 0)]
            fits = stray & (used < HOPS)

            @pl.when(fits)
            def _():
                counts[home] = used + 1
                pltpu.make_async_copy(
                    received.at[i, pl.ds(pl.multiple_of(j * BR, BR), BR)],
                    out.at[home, pl.ds(pl.multiple_of(used * BR, BR), BR)],
                    sem,
                ).start()
                target = index[i, 0, j].astype(jnp.float32)
                marks[home] = jnp.where(lane == used, target, marks[home])

            return (
                missed + jnp.where(stray & (used >= HOPS), 1, 0),
                sent + jnp.where(fits, 1, 0),
            )

        count = jnp.where(index[i, 0, STRAY_LANE] > 0, index[i, 0, COUNT_LANE], 0)
        return lax.fori_loop(0, count, slot, carry)

    missed, sent = lax.fori_loop(0, PEERS, source, (jnp.int32(0), jnp.int32(0)))
    write_tags(marks, tags, counts, None, missed, GROUPS)
    tag_copy = pltpu.make_async_copy(tags, out.at[:, pl.ds(HOPS * BR, LABEL_ROWS)], tag_sem)
    tag_copy.start()

    def drain(i, carry):
        pltpu.make_async_copy(received.at[0, pl.ds(0, BR)], out.at[0, pl.ds(0, BR)], sem).wait()
        return carry

    lax.fori_loop(0, sent, drain, 0)
    tag_copy.wait()


def forward(index, received):
    return pl.pallas_call(
        forward_kernel,
        out_shape=jax.ShapeDtypeStruct((GROUPS, HOPS * BR + LABEL_ROWS, 128), jnp.bfloat16),
        in_specs=[
            pl.BlockSpec(memory_space=pltpu.SMEM),
            pl.BlockSpec(memory_space=pl.ANY),
        ],
        out_specs=pl.BlockSpec(memory_space=pl.ANY),
        scratch_shapes=[
            pltpu.VMEM((GROUPS, 8, 128), jnp.float32),
            pltpu.VMEM((GROUPS, LABEL_ROWS, 128), jnp.bfloat16),
            pltpu.SMEM((GROUPS,), jnp.int32),
            pltpu.SemaphoreType.DMA,
            pltpu.SemaphoreType.DMA,
        ],
        compiler_params=pltpu.CompilerParams(vmem_limit_bytes=2 << 20),
        name="forward",
    )(index, received)


def gather_kernel(index, late_index, received, late, out, total, landed, sems, sem):
    def fetch_from(array, labels, first):
        def fetch(i, at):
            def slot(j, spot):
                pltpu.make_async_copy(
                    array.at[i, pl.ds(pl.multiple_of(j * BR, BR), BR)],
                    landed.at[spot],
                    sems.at[first + i],
                ).start()
                return spot + 1

            return lax.fori_loop(0, labels[i, 0, COUNT_LANE], slot, at)

        return fetch

    def add_from(array, labels, first):
        def source(i, carry):
            missed, at = carry
            count = labels[i, 0, COUNT_LANE]

            def arrive(j, carry):
                pltpu.make_async_copy(
                    array.at[0, pl.ds(0, BR)], landed.at[0], sems.at[first + i]
                ).wait()
                return carry

            lax.fori_loop(0, count, arrive, 0)

            def slot(j, spot):
                target = labels[i, 0, j]
                chunk = target // OWNED
                row = target - chunk * OWNED
                start = row * BR + jnp.where(row >= 2, FLAG_ROWS, 0)
                chunk = jnp.where(labels[i, 0, HOP_LANE + j] >= 0, 16, chunk)
                start = pl.multiple_of(start, 8)
                total[chunk, pl.ds(start, BR), :] += landed[spot].astype(jnp.float32)
                return spot + 1

            at = lax.fori_loop(0, count, slot, at)
            return missed + labels[i, 0, OVER_LANE], at

        return source

    at = lax.fori_loop(0, PEERS, fetch_from(received, index, 0), jnp.int32(0))
    lax.fori_loop(0, GROUPS, fetch_from(late, late_index, PEERS), at)
    total[0:16] = jnp.zeros((16, CHUNK, 128), jnp.float32)
    carry = (jnp.int32(0), jnp.int32(0))
    carry = lax.fori_loop(0, PEERS, add_from(received, index, 0), carry)
    missed, _ = lax.fori_loop(0, GROUPS, add_from(late, late_index, PEERS), carry)
    total[0:16, PIVOT_ROWS : PIVOT_ROWS + FLAG_ROWS, :] = jnp.full(
        (16, FLAG_ROWS, 128), missed.astype(jnp.float32)
    )
    copy = pltpu.make_async_copy(total.at[pl.ds(0, 16)], out, sem)
    copy.start()
    copy.wait()


def add_up(index, late_index, received, late):
    smem = pl.BlockSpec(memory_space=pltpu.SMEM)
    anywhere = pl.BlockSpec(memory_space=pl.ANY)
    return pl.pallas_call(
        gather_kernel,
        out_shape=jax.ShapeDtypeStruct((16, CHUNK, 128), jnp.float32),
        in_specs=[smem, smem, anywhere, anywhere],
        out_specs=anywhere,
        scratch_shapes=[
            pltpu.VMEM((17, CHUNK, 128), jnp.float32),
            pltpu.VMEM((PEERS * SLOTS + GROUPS * HOPS, BR, 128), jnp.bfloat16),
            pltpu.SemaphoreType.DMA((PEERS + GROUPS,)),
            pltpu.SemaphoreType.DMA,
        ],
        compiler_params=pltpu.CompilerParams(vmem_limit_bytes=20 << 20),
        name="add_up",
    )(index, late_index, received, late)


def solve_kernel(spot, pivots, rhs, *refs):
    lowers, inverses = refs[0:4], refs[4:8]
    owned, update, solved_out, update_out, lower, inverse, kept = refs[8:]
    chain_at = spot[0]
    live_count = pivots[0]
    for shift in range(4):
        block = (chain_at - shift) & 3
        lower[block] = lowers[shift][...]
        inverse[block] = inverses[shift][...]
    for block in range(4):
        rows = slice(block * 256, (block + 1) * 256)
        at = block * (PIVOT_ROWS + FLAG_ROWS)
        partial = rhs[at : at + PIVOT_ROWS, :]
        if block > 0:
            partial = partial - jnp.dot(
                lower[block, :, 0 : block * 256],
                kept[0 : block * 256, :],
                preferred_element_type=jnp.float32,
            )
        row = block * 256 + lax.broadcasted_iota(jnp.int32, (256, 128), 0)
        product = jnp.dot(
            inverse[block],
            partial,
            precision=lax.Precision.HIGHEST,
            preferred_element_type=jnp.float32,
        )
        here = jnp.where(row < live_count, product, 0.0)
        kept[rows, :] = here.astype(jnp.bfloat16)

        @pl.when(chain_at == block)
        def _():
            solved_out[...] = here

    update_out[...] = owned[PIVOT_ROWS + FLAG_ROWS :, :] - jnp.dot(
        update[...], kept[...], preferred_element_type=jnp.float32
    )


def solve(spot, pivots, rhs, lowers, inverses, owned, update):
    smem = pl.BlockSpec(memory_space=pltpu.SMEM)
    vmem = pl.BlockSpec(memory_space=pltpu.VMEM)
    return pl.pallas_call(
        solve_kernel,
        out_shape=(
            jax.ShapeDtypeStruct((256, 128), jnp.float32),
            jax.ShapeDtypeStruct((512, 128), jnp.float32),
        ),
        in_specs=[smem, smem] + [vmem] * 11,
        out_specs=(vmem, vmem),
        scratch_shapes=[
            pltpu.VMEM((4, 256, 768), jnp.bfloat16),
            pltpu.VMEM((4, 256, 256), jnp.float32),
            pltpu.VMEM((1024, 128), jnp.bfloat16),
        ],
        compiler_params=pltpu.CompilerParams(vmem_limit_bytes=20 << 20),
        name="solve",
    )(spot, pivots, rhs, *lowers, *inverses, owned, update)


def around_chain(value):
    moved = [
        lax.ppermute(value, "chain", [(i, (i + shift) % 4) for i in range(4)])
        for shift in (1, 2, 3)
    ]
    return (value, *moved)


def labels_of(received):
    return received[:, -LABEL_ROWS : 1 - LABEL_ROWS, :].astype(jnp.int32)


def body(
    rhs, child_blocks, dest_front, dest_place, front_pivots, diag_inv, lower_factor, update_factor
):
    fronts = dest_front.reshape(-1)
    spot = lax.axis_index("chain").astype(jnp.int32).reshape(1)
    turn = lax.axis_index(LINE).astype(jnp.int32).reshape(1) + 2 * spot
    packed = pack(turn, fronts, dest_place, child_blocks)
    received = lax.all_to_all(packed, SLAB, split_axis=0, concat_axis=0, tiled=True)
    index = labels_of(received)
    late = lax.all_to_all(forward(index, received), LINE, split_axis=0, concat_axis=0, tiled=True)
    dense = add_up(index, labels_of(late), received, late)
    dense, lower_factor, diag_inv = lax.optimization_barrier((dense, lower_factor, diag_inv))
    owned = lax.psum_scatter(dense, "z", scatter_dimension=0, tiled=True)
    owned = lax.optimization_barrier(owned).reshape(CHUNK, 128)
    lowers = around_chain(lower_factor)
    inverses = around_chain(diag_inv)

    def share(mine):
        padded = jnp.pad(rhs, ((0, FLAG_ROWS), (0, 0)))
        return lax.all_gather(
            padded + mine[: PIVOT_ROWS + FLAG_ROWS], "chain", axis=0, tiled=True
        )

    def finish(all_rhs, mine):
        return solve(spot, front_pivots, all_rhs, lowers, inverses, mine, update_factor)

    def general(all_rhs, mine):
        blocks = full_exchange(child_blocks, fronts, dest_place).reshape(OWNED * BR, 128)
        flags = jnp.zeros((FLAG_ROWS, 128), jnp.float32)
        mine = jnp.concatenate([blocks[:PIVOT_ROWS], flags, blocks[PIVOT_ROWS:]])
        return finish(share(mine), mine)

    all_rhs = share(owned)
    over = jnp.sum(all_rhs.reshape(4, PIVOT_ROWS + FLAG_ROWS, 128)[:, PIVOT_ROWS, 0])
    return lax.cond(over > 0, general, finish, all_rhs, owned)


def solution(mesh):
    grid = Mesh(mesh.devices.reshape(4, 16, 2, 4), ALL)
    rows = P(ALL, None)
    return jax.shard_map(
        body,
        mesh=grid,
        in_specs=(rows, P(ALL, None, None), rows, P(ALL), P(FRONT), rows, rows, rows),
        out_specs=(rows, rows),
        check_vma=False,
    )
```

time: 286 us -> 247 us (0.86)
  blocking collectives: 153 us -> 108 us
  Pallas kernels: 19.6 us -> 25 us
    all_to_all x1, blocking collectives: 139 us -> 70.5 us  [body(): lax.all_to_all(packed, SLAB, split_axis=0, concat_axis=0, tiled=True)]
    all_to_all x0 -> x1, blocking collectives: none -> 24.6 us  [body(): lax.all_to_all(forward(index, received), LINE, split_axis=0, concat_axis=...]
    ppermute x6, waiting for transfers between devices: 0.02 us -> 18.5 us  [around_chain(): lax.ppermute(value, 'chain', [(i, (i + shift) % 4) for i in range(4)])]
    unnamed x2, waiting for transfers between devices: 69.1 us -> 52.8 us
    pallas_call x1, Pallas kernels: 4.8 us -> 8.32 us  [pack(): pl.pallas_call(send_kernel, out_shape=jax.ShapeDtypeStruct((PEERS, SLOTS...]
  transfers between devices with their start and end apart: 7 -> 7, of which waited for: 1 -> 3; matrix products, arithmetic and copies ran while one was open for 0% -> 0% of each run, Pallas kernels for 0% -> 0%
where the time goes in v3:
time: 247 us
  blocking collectives  108 us (44%)
  waiting for transfers between devices  71.4 us (29%)
  Pallas kernels  25 us (10%)
  starting transfers between devices  20.9 us (8%)
  between operations  14.9 us (6%)
  local copies, waits for them, and re-layouts  4.39 us (2%)
    all_to_all x1, blocking collectives, body(): lax.all_to_all(packed, SLAB, split_axis=0, concat_axis=0, tiled=True)  70.5 us
    unnamed x2, waiting for transfers between devices  52.8 us
    all_to_all x1, blocking collectives, body(): lax.all_to_all(forward(index, received), LINE, split_axis=0, concat_axis=...  24.6 us
    ppermute x6, starting transfers between devices, around_chain(): lax.ppermute(value, 'chain', [(i, (i + shift) % 4) for i in range(4)])  20.8 us
    ppermute x6, waiting for transfers between devices, around_chain(): lax.ppermute(value, 'chain', [(i, (i + shift) % 4) for i in range(4)])  18.5 us
    all_gather x1, blocking collectives, share(): lax.all_gather(padded + mine[:PIVOT_ROWS + FLAG_ROWS], 'chain', axis=0, t...  13.2 us
    pallas_call x1, Pallas kernels, pack(): pl.pallas_call(send_kernel, out_shape=jax.ShapeDtypeStruct((PEERS, SLOTS...  8.32 us
    pallas_call x1, Pallas kernels, add_up(): pl.pallas_call(gather_kernel, out_shape=jax.ShapeDtypeStruct((16, CHUNK,...  8.1 us
  transfers between devices with their start and end apart: 7, of which 3 were waited for; matrix products, arithmetic and copies ran while one was open for 0% of the time, Pallas kernels for 0%

profile of v3, /device:TPU:6, one launch (start us, length us, event | category | flops | bytes accessed | tf_op | source)
XLA Modules:
  0.0 246.5 jit_solution(17600896292138356782)
XLA Ops:
  7.2 0.0 reduce-scatter.7.cloned.1.call-start
  7.2 8.3 %pack.1 = bf16[32,656,128]{2,1,0:T(8,128)(2,1)S(1)} custom-call(s32[1]{0:T(128)S(6)} %add.93.spot, s32[88]{0:T(128)} %bitcast.27, s32[88]{0:T(128)} %place.1, bf16[88,128,128]{2,1,0:T(8,128)(2,1)} %blocks.1), custom_call_target="tpu_custom_call" | custom-call | tf_op jit(solution)/shard_map/pack/pallas_call | solution.py:154
  15.5 70.5 %all_to_all.19.received = bf16[32,656,128]{2,1,0:T(8,128)(2,1)S(1)} all-to-all(bf16[32,656,128]{2,1,0:T(8,128)(2,1)S(1)} %pack.1), channel_id=1, replica_groups=mesh['x'=4,'z'=16,'core'=2,'chain'=4] {'x','core','chain'}, dimensions={0} | all-to-all | bytes 10747904 | tf_op jit(solution)/shard_map/all_to_all | solution.py:394
  86.1 1.4 forward.1
  87.5 24.6 %all_to_all.20.late = bf16[8,784,128]{2,1,0:T(8,128)(2,1)S(1)} all-to-all(bf16[8,784,128]{2,1,0:T(8,128)(2,1)S(1)} %forward.1), channel_id=1, replica_groups=mesh['x'=4,'z'=16,'core'=2,'chain'=4] {'x','core'}, dimensions={0} | all-to-all | bytes 3211264 | tf_op jit(solution)/shard_map/all_to_all | solution.py:396
  112.1 0.0 copy-start.4
  112.1 0.0 copy-start.1
  112.2 0.0 copy-start.2
  112.2 0.0 copy-start.20
  112.2 8.1 %add_up.1 = f32[16,776,128]{2,1,0:T(8,128)S(1)} custom-call(s32[32,1,128]{2,1,0:T(1,128)S(1)} %slice_convert_fusion.index, s32[8,1,128]{2,1,0:T(1,128)S(1)} %slice_convert_fusion.1.late_index, bf16[32,656,128]{2,1,0:T(8,128)(2,1)S(1)} %all_to_all.19.received, bf16[8,784,128]{2,1,0:T(8,128)(2,1)S(1)} %all_to_all.20.late), custom_call_target="tpu_custom_call" | custom-call | tf_op jit(solution)/shard_map/add_up/pallas_call | solution.py:300
  120.3 2.7 %copy-done = f32[16,776,128]{2,1,0:T(8,128)} copy-done((f32[16,776,128]{2,1,0:T(8,128)}, f32[16,776,128]{2,1,0:T(8,128)S(1)}, u32[]{:S(2)}) %copy-start) | copy-done | bytes 6357016
  123.0 0.0 reduce-scatter.7.cloned.1.call-update
  123.0 2.6 %collective-permute-start.3 = (f32[256,256]{1,0:T(8,128)S(1)}, f32[256,256]{1,0:T(8,128)S(1)}, u32[]{:S(2)}, u32[]{:S(2)}) collective-permute-start(f32[256,256]{1,0:T(8,128)S(1)} %copy-done.12), channel_id=1, source_target_pairs={{0,1},{1,2},{2,3},{3,0},{4,5},{5,6},{6,7},{7,4},{8,9},{9,10},{10,1... | collective-permute-start | bytes 786440 | tf_op jit(solution)/shard_map/ppermute | solution.py:377
  125.6 3.3 %collective-permute-start = (bf16[256,768]{1,0:T(8,128)(2,1)S(1)}, bf16[256,768]{1,0:T(8,128)(2,1)S(1)}, u32[]{:S(2)}, u32[]{:S(2)}) collective-permute-start(bf16[256,768]{1,0:T(8,128)(2,1)S(1)} %copy-done.4), channel_id=1, source_target_pairs={{0,1},{1,2},{2,3},{3,0},{4,5},{5,6},{6,7},{7,4},{8,9},{9,10},{10,1... | collective-permute-start | bytes 1179656 | tf_op jit(solution)/shard_map/ppermute | solution.py:377
  128.9 4.5 %collective-permute-start.1 = (bf16[256,768]{1,0:T(8,128)(2,1)S(1)}, bf16[256,768]{1,0:T(8,128)(2,1)S(1)}, u32[]{:S(2)}, u32[]{:S(2)}) collective-permute-start(bf16[256,768]{1,0:T(8,128)(2,1)S(1)} %copy-done.4), channel_id=1, source_target_pairs={{0,2},{1,3},{2,0},{3,1},{4,6},{5,7},{6,4},{7,5},{8,10},{9,11},{10,... | collective-permute-start | bytes 1179656 | tf_op jit(solution)/shard_map/ppermute | solution.py:377
  133.4 3.2 %collective-permute-start.2 = (bf16[256,768]{1,0:T(8,128)(2,1)S(1)}, bf16[256,768]{1,0:T(8,128)(2,1)S(1)}, u32[]{:S(2)}, u32[]{:S(2)}) collective-permute-start(bf16[256,768]{1,0:T(8,128)(2,1)S(1)} %copy-done.4), channel_id=1, source_target_pairs={{0,3},{1,0},{2,1},{3,2},{4,7},{5,4},{6,5},{7,6},{8,11},{9,8},{10,9... | collective-permute-start | bytes 1179656 | tf_op jit(solution)/shard_map/ppermute | solution.py:377
  136.7 2.7 %collective-permute-start.4 = (f32[256,256]{1,0:T(8,128)S(1)}, f32[256,256]{1,0:T(8,128)S(1)}, u32[]{:S(2)}, u32[]{:S(2)}) collective-permute-start(f32[256,256]{1,0:T(8,128)S(1)} %copy-done.12), channel_id=1, source_target_pairs={{0,2},{1,3},{2,0},{3,1},{4,6},{5,7},{6,4},{7,5},{8,10},{9,11},{10,... | collective-permute-start | bytes 786440 | tf_op jit(solution)/shard_map/ppermute | solution.py:377
  139.4 4.5 %collective-permute-start.5 = (f32[256,256]{1,0:T(8,128)S(1)}, f32[256,256]{1,0:T(8,128)S(1)}, u32[]{:S(2)}, u32[]{:S(2)}) collective-permute-start(f32[256,256]{1,0:T(8,128)S(1)} %copy-done.12), channel_id=1, source_target_pairs={{0,3},{1,0},{2,1},{3,2},{4,7},{5,4},{6,5},{7,6},{8,11},{9,8},{10,9... | collective-permute-start | bytes 786440 | tf_op jit(solution)/shard_map/ppermute | solution.py:377
  143.9 14.0 %collective-permute-done.4 = f32[256,256]{1,0:T(8,128)S(1)} collective-permute-done((f32[256,256]{1,0:T(8,128)S(1)}, f32[256,256]{1,0:T(8,128)S(1)}, u32[]{:S(2)}, u32[]{:S(2)}) %collective-permute-start.4) | collective-permute-done | bytes 262176 | tf_op jit(solution)/shard_map/ppermute | solution.py:377
  157.9 4.6 %collective-permute-done.5 = f32[256,256]{1,0:T(8,128)S(1)} collective-permute-done((f32[256,256]{1,0:T(8,128)S(1)}, f32[256,256]{1,0:T(8,128)S(1)}, u32[]{:S(2)}, u32[]{:S(2)}) %collective-permute-start.5) | collective-permute-done | bytes 262176 | tf_op jit(solution)/shard_map/ppermute | solution.py:377
  162.5 0.0 collective-permute-done
  162.5 0.0 collective-permute-done.1
  162.5 0.6 copy-done.18
  163.2 0.1 copy-done.6
  163.3 0.2 copy-done.8
  163.4 0.8 copy-done.10
  164.2 52.8 %reduce-scatter.7.cloned.1.call-done = f32[1,776,128]{2,1,0:T(8,128)} async-done(((f32[16,776,128]{2,1,0:T(8,128)}), f32[1,776,128]{2,1,0:T(8,128)}) %reduce-scatter.7.cloned.1.call-update) | async-done | bytes 397328
  217.0 1.0 fusion.10
  218.0 13.2 %all_gather.6 = f32[1056,128]{1,0:T(8,128)S(1)} all-gather(f32[264,128]{1,0:T(8,128)S(1)} %fusion.10), channel_id=1, replica_groups=mesh['x'=4,'z'=16,'core'=2,'chain'=4] {'chain'}, dimensions={0}, use_global_device_ids=true | all-gather | bytes 675840 | tf_op jit(solution)/shard_map/all_gather | solution.py:406
  231.2 0.6 slice_reduce_fusion
  232.5 7.2 %conditional.1 = ((f32[256,128]{1,0:T(8,128)}, f32[512,128]{1,0:T(8,128)})) conditional(s32[]{:T(128)} %convert_element_type.18, (f32[1,776,128]{2,1,0:T(8,128)}, s32[1]{0:T(128)}, s32[1]{0:T(128)}, f32[1056,128]{1,0:T(8,128)S(1)}, bf16[256,768]{1,0:T(8,128)(2,1)}, /*index=5*/bf16[256,768]{1,0:T(8,128)(2,1)}, bf16[256,768]{1,0:T(8,128)(2,1)}, ...), branch_computations={%region_2.3_spmd, %region_3.7_spmd} | conditional | flops 205814176 | bytes 128252512 | solution.py:421
  232.5 7.2 %solve.2 = (f32[256,128]{1,0:T(8,128)}, f32[512,128]{1,0:T(8,128)}) custom-call(s32[1]{0:T(128)} %get-tuple-element.59.spot, s32[1]{0:T(128)} %get-tuple-element.60.pivots, f32[1056,128]{1,0:T(8,128)S(1)} %get-tuple-element.61.rhs, bf16[256,768]{1,0:T(8,128)(2,1)} %get-tuple-element.62.refs_0_, bf16[256,768]{1,0:T(8,128)(2,1)} %get-tuple-element.63.refs_1_, ...), custom_call_target="tpu_custom_call" | custom-call | tf_op jit(solution)/shard_map/cond/branch_0_fun/solve/pallas_call | solution.py:357
  (19 shorter events, 0.1 us)
Async XLA Ops:
  7.2 209.9 %reduce-scatter.7.cloned.1.call-start = ((), (), s32[]{:S(2)}) async-start(), calls=%async_computation.7 | async-start | bytes 6754304
  112.1 10.9 %copy-start.12 = (f32[256,256]{1,0:T(8,128)S(1)}, f32[256,256]{1,0:T(8,128)}, u32[]{:S(2)}) copy-start(f32[256,256]{1,0:T(8,128)} %param.15) | copy-start | bytes 786436
  112.1 13.4 %copy-start.4 = (bf16[256,768]{1,0:T(8,128)(2,1)S(1)}, bf16[256,768]{1,0:T(8,128)(2,1)}, u32[]{:S(2)}) copy-start(bf16[256,768]{1,0:T(8,128)(2,1)} %param.16) | copy-start | bytes 1179652
  112.1 120.3 %copy-start.1 = (s32[88]{0:T(128)S(1)}, s32[88]{0:T(128)}, u32[]{:S(2)}) copy-start(s32[88]{0:T(128)} %place.1) | copy-start | bytes 1060
  112.2 120.3 %copy-start.2 = (bf16[88,128,128]{2,1,0:T(8,128)(2,1)S(1)}, bf16[88,128,128]{2,1,0:T(8,128)(2,1)}, u32[]{:S(2)}) copy-start(bf16[88,128,128]{2,1,0:T(8,128)(2,1)} %blocks.1) | copy-start | bytes 8650756
  112.2 120.3 %copy-start.20 = (s32[88,1]{0,1:T(1,128)S(1)}, s32[88,1]{0,1:T(1,128)}, u32[]{:S(2)}) copy-start(s32[88,1]{0,1:T(1,128)} %param.12) | copy-start | bytes 1060
  120.3 2.7 %copy-start = (f32[16,776,128]{2,1,0:T(8,128)}, f32[16,776,128]{2,1,0:T(8,128)S(1)}, u32[]{:S(2)}) copy-start(f32[16,776,128]{2,1,0:T(8,128)S(1)} %add_up.1) | copy-start | bytes 19070980
  123.0 16.4 %collective-permute-start.3 = (f32[256,256]{1,0:T(8,128)S(1)}, f32[256,256]{1,0:T(8,128)S(1)}, u32[]{:S(2)}, u32[]{:S(2)}) collective-permute-start(f32[256,256]{1,0:T(8,128)S(1)} %copy-done.12), channel_id=1, source_target_pairs={{0,1},{1,2},{2,3},{3,0},{4,5},{5,6},{6,7},{7,4},{8,9},{9,10},{10,1... | collective-permute-start | bytes 786440 | tf_op jit(solution)/shard_map/ppermute | solution.py:377
  125.6 36.9 %collective-permute-start = (bf16[256,768]{1,0:T(8,128)(2,1)S(1)}, bf16[256,768]{1,0:T(8,128)(2,1)S(1)}, u32[]{:S(2)}, u32[]{:S(2)}) collective-permute-start(bf16[256,768]{1,0:T(8,128)(2,1)S(1)} %copy-done.4), channel_id=1, source_target_pairs={{0,1},{1,2},{2,3},{3,0},{4,5},{5,6},{6,7},{7,4},{8,9},{9,10},{10,1... | collective-permute-start | bytes 1179656 | tf_op jit(solution)/shard_map/ppermute | solution.py:377
  128.9 33.5 %collective-permute-start.1 = (bf16[256,768]{1,0:T(8,128)(2,1)S(1)}, bf16[256,768]{1,0:T(8,128)(2,1)S(1)}, u32[]{:S(2)}, u32[]{:S(2)}) collective-permute-start(bf16[256,768]{1,0:T(8,128)(2,1)S(1)} %copy-done.4), channel_id=1, source_target_pairs={{0,2},{1,3},{2,0},{3,1},{4,6},{5,7},{6,4},{7,5},{8,10},{9,11},{10,... | collective-permute-start | bytes 1179656 | tf_op jit(solution)/shard_map/ppermute | solution.py:377
  133.4 29.0 %collective-permute-start.2 = (bf16[256,768]{1,0:T(8,128)(2,1)S(1)}, bf16[256,768]{1,0:T(8,128)(2,1)S(1)}, u32[]{:S(2)}, u32[]{:S(2)}) collective-permute-start(bf16[256,768]{1,0:T(8,128)(2,1)S(1)} %copy-done.4), channel_id=1, source_target_pairs={{0,3},{1,0},{2,1},{3,2},{4,7},{5,4},{6,5},{7,6},{8,11},{9,8},{10,9... | collective-permute-start | bytes 1179656 | tf_op jit(solution)/shard_map/ppermute | solution.py:377
  136.7 21.2 %collective-permute-start.4 = (f32[256,256]{1,0:T(8,128)S(1)}, f32[256,256]{1,0:T(8,128)S(1)}, u32[]{:S(2)}, u32[]{:S(2)}) collective-permute-start(f32[256,256]{1,0:T(8,128)S(1)} %copy-done.12), channel_id=1, source_target_pairs={{0,2},{1,3},{2,0},{3,1},{4,6},{5,7},{6,4},{7,5},{8,10},{9,11},{10,... | collective-permute-start | bytes 786440 | tf_op jit(solution)/shard_map/ppermute | solution.py:377
  139.4 23.1 %copy-start.14 = (f32[256,256]{1,0:T(8,128)}, f32[256,256]{1,0:T(8,128)S(1)}, u32[]{:S(2)}) copy-start(f32[256,256]{1,0:T(8,128)S(1)} %collective-permute-done.3) | copy-start | bytes 786436
  139.4 23.0 %collective-permute-start.5 = (f32[256,256]{1,0:T(8,128)S(1)}, f32[256,256]{1,0:T(8,128)S(1)}, u32[]{:S(2)}, u32[]{:S(2)}) collective-permute-start(f32[256,256]{1,0:T(8,128)S(1)} %copy-done.12), channel_id=1, source_target_pairs={{0,3},{1,0},{2,1},{3,2},{4,7},{5,4},{6,5},{7,6},{8,11},{9,8},{10,9... | collective-permute-start | bytes 786440 | tf_op jit(solution)/shard_map/ppermute | solution.py:377
  157.9 4.6 %copy-start.16 = (f32[256,256]{1,0:T(8,128)}, f32[256,256]{1,0:T(8,128)S(1)}, u32[]{:S(2)}) copy-start(f32[256,256]{1,0:T(8,128)S(1)} %collective-permute-done.4) | copy-start | bytes 786436
  162.5 0.7 copy-start.18
  162.5 0.8 copy-start.6
  162.5 1.0 copy-start.8
  163.4 0.8 copy-start.10
Sparse Core Ops, SparseCore 0:
  123.1 93.8 reduce-scatter.6
